TPU v7x, 256 devices: a whole 4x4x8 slice. The times are simulated.
256 devices in a mesh: dp: 8 (over z_lo, x), space: 32 (over y, z_hi, core).
Axes of the slice: x: 4, y: 4, z: 8 (z_hi: 4, z_lo: 2; z = z_hi * 2 + z_lo), core: 2. Of those that a mesh axis runs over, the one named last changes fastest.
Arguments:
- images: bfloat16 [8, 32, 96, 64, 128], P('dp', 'space'), may hold values from -60 to 60
- first_weight: bfloat16 [3, 3, 128, 256], replicated, may hold values from -0.1875 to 0.1875
- norm_gain: float32 [256], replicated, may hold values from 0.5 to 2
- norm_bias: float32 [256], replicated, may hold values from -2 to 2
- second_weight: bfloat16 [3, 3, 256, 256], replicated, may hold values from -0.125 to 0.125
- upstream: bfloat16 [8, 32, 48, 32, 256], P('dp', 'space'), may hold values from -45 to 45
Outputs:
- input_grad: bfloat16 [8, 32, 96, 64, 128], P('dp', 'space')
- first_grad: float32 [3, 3, 128, 256], replicated
- second_grad: float32 [3, 3, 256, 256], replicated
- gain_grad: float32 [256], replicated
- bias_grad: float32 [256], replicated
All inputs are finite; a program needn't handle non-finite values.
Results may differ from a plain program's by a relative error of at most 0.0049.
Values may be sent and summed in bfloat16 or wider, within the bound.
A program may use at most 64 MiB of HBM per device.

v0:
```python
import jax
import jax.numpy as jnp
from jax import lax
from jax.experimental import pallas as pl
from jax.experimental.pallas import tpu as pltpu
from jax.sharding import PartitionSpec as P

F32 = jnp.float32
BF16 = jnp.bfloat16
MESH = pl.DeviceIdType.MESH

TH = 48
TW = 32
CIN = 128
CMID = 256
PIX = TH * TW
TILES = 32
GSIZE = 8
SPACE_OFFSETS = (1, -1, 3, -3, 4, -4, 5, -5)


def dot(a, b):
    return jnp.dot(a, b, preferred_element_type=F32)


def dot_t(a, b):
    return lax.dot_general(a, b, (((1,), (1,)), ((), ())), preferred_element_type=F32)


def group_sum(value):
    lane = lax.broadcasted_iota(jnp.int32, value.shape, 1)
    for step in (1, 2, 4):
        up = pltpu.roll(value, step, 1)
        down = pltpu.roll(value, value.shape[1] - step, 1)
        value = value + jnp.where((lane & step) != 0, up, down)
    return value


def kernel(
    x, w1, gain, bias, w2, g,
    ig, og1, og2, ogb,
    xf, re, ro, xs, xl, xtop,
    gs, gf, gfirst, glast, rl, rr,
    zb, ab, act_t,
    cgf, c0, c1, cs, cr, igf,
    sa, sb, ta, tb, ux, uz,
    p2, cc2, s2, rx2, q2, rz2, rc2, az2, ax2,
    p1, cc1, s1, rx1, q1, rz1, rc1, az1, ax1,
    h_send, h_recv, c_send, c_recv,
    sa_send, sa_recv, sb_send, sb_recv,
    ta_send, ta_recv, tb_send, tb_recv,
    ux_send, ux_recv, uz_send, uz_recv,
    r2_send, r2_recv, r1_send, r1_recv,
):
    dp = lax.axis_index("dp")
    sp = lax.axis_index("space")
    core = lax.rem(sp, 2)
    z_hi = lax.rem(sp // 2, 4)
    y = sp // 8
    xx = lax.rem(dp, 4)
    z_lo = dp // 4
    z = z_hi * 2 + z_lo
    position = lax.rem(sp + 6, TILES)
    column = lax.rem(position, 4)
    tile_row = position // 4
    first_col, last_col = column == 0, column == 3
    first_row, last_row = tile_row == 0, tile_row == TILES // 4 - 1

    def at_space(offset):
        return (dp, lax.rem(sp + offset + TILES, TILES))

    def at_chip(x_, y_, z_, core_):
        return (lax.rem(z_, 2) * 4 + x_, (y_ * 4 + z_ // 2) * 2 + core_)

    def at_plane(k):
        return at_chip(lax.rem(xx + k % 4, 4), lax.rem(y + k // 4, 4), z, core)

    def at_z(k):
        return at_chip(xx, y, lax.rem(z + k, 8), core)

    def at_core_y(k):
        return at_chip(xx, lax.rem(y + k // 2, 4), z, lax.rem(core + k % 2, 2))

    partner = at_chip(xx, y, z, 1 - core)

    barrier = pltpu.get_barrier_semaphore()
    greeted = 0
    for offset in SPACE_OFFSETS:
        pl.semaphore_signal(barrier, inc=1, device_id=at_space(offset), device_id_type=MESH)
        greeted += 1
    for k in range(1, 16):
        pl.semaphore_signal(barrier, inc=1, device_id=at_plane(k), device_id_type=MESH)
        greeted += 1
    for k in range(1, 8):
        pl.semaphore_signal(barrier, inc=1, device_id=at_z(k), device_id_type=MESH)
        greeted += 1
    for k in range(1, 8):
        pl.semaphore_signal(barrier, inc=1, device_id=at_core_y(k), device_id_type=MESH)
        greeted += 1

    pending = []

    def send(src, dst, send_sem, recv_sem, device):
        copy = pltpu.make_async_remote_copy(
            src_ref=src, dst_ref=dst, send_sem=send_sem, recv_sem=recv_sem,
            device_id=device, device_id_type=MESH,
        )
        copy.start()
        pending.append(copy)
        return copy

    def arrive(copies):
        for copy in copies:
            copy.wait_recv()

    xs[...] = x[:, 48:64, :].astype(F32)[:, 15:16, :]

    def widen_g(p, carry):
        value = g[p]
        gs[1, p + 1] = value
        gf[p + 1, 8:40, :] = value.astype(F32)
        return carry

    lax.fori_loop(0, TH, widen_g, 0)
    gfirst[...] = gf[1 : TH + 1, 8:9, :]
    glast[...] = gf[1 : TH + 1, 39:40, :]

    pl.semaphore_wait(barrier, greeted)

    halo = [
        send(xs, xl.at[pl.ds(1, 2 * TH)], h_send.at[0], h_recv.at[0], at_space(1)),
        send(xs.at[2 * TH - 1], xl.at[0], h_send.at[1], h_recv.at[1], at_space(5)),
        send(x.at[2 * TH - 1], xtop, h_send.at[2], h_recv.at[2], at_space(4)),
        send(glast, rl.at[pl.ds(1, TH)], h_send.at[3], h_recv.at[3], at_space(1)),
        send(glast.at[TH - 1], rl.at[0], h_send.at[4], h_recv.at[4], at_space(5)),
        send(glast.at[0], rl.at[TH + 1], h_send.at[5], h_recv.at[5], at_space(-3)),
        send(gfirst, rr.at[pl.ds(1, TH)], h_send.at[6], h_recv.at[6], at_space(-1)),
        send(gfirst.at[TH - 1], rr.at[0], h_send.at[7], h_recv.at[7], at_space(3)),
        send(gfirst.at[0], rr.at[TH + 1], h_send.at[8], h_recv.at[8], at_space(-5)),
        send(g.at[TH - 1], gs.at[1, 0], h_send.at[9], h_recv.at[9], at_space(4)),
        send(g.at[0], gs.at[1, TH + 1], h_send.at[10], h_recv.at[10], at_space(-4)),
    ]

    def split_x(p, carry):
        xf[2 * p + 1, 8:72, :] = x[2 * p].astype(F32)
        xf[2 * p + 2, 8:72, :] = x[2 * p + 1].astype(F32)
        re[p, :, 128:256] = xf[2 * p + 1, pl.ds(8, TW, stride=2), :].astype(BF16)
        re[p, :, 256:384] = xf[2 * p + 1, pl.ds(9, TW, stride=2), :].astype(BF16)
        ro[p + 1, :, 128:256] = xf[2 * p + 2, pl.ds(8, TW, stride=2), :].astype(BF16)
        ro[p + 1, :, 256:384] = xf[2 * p + 2, pl.ds(9, TW, stride=2), :].astype(BF16)
        return carry

    lax.fori_loop(0, TH, split_x, 0)

    arrive(halo)
    xf[0, 8:72, :] = jnp.where(first_row, 0.0, xtop[...].astype(F32))
    xf[:, 7:8, :] = jnp.where(first_col, 0.0, xl[...])
    xf[0, 7:8, :] = jnp.where(jnp.logical_or(first_col, first_row), 0.0, xl[0])
    ro[0, :, 128:256] = xf[0, pl.ds(8, TW, stride=2), :].astype(BF16)
    ro[0, :, 256:384] = xf[0, pl.ds(9, TW, stride=2), :].astype(BF16)

    def left_x(p, carry):
        re[p, :, 0:128] = xf[2 * p + 1, pl.ds(7, TW, stride=2), :].astype(BF16)
        ro[p, :, 0:128] = xf[2 * p, pl.ds(7, TW, stride=2), :].astype(BF16)
        return carry

    lax.fori_loop(0, TH, left_x, 0)
    ro[TH, :, 0:128] = xf[2 * TH, pl.ds(7, TW, stride=2), :].astype(BF16)

    top = jnp.where(first_row, 0.0, gs[1, 0].astype(F32))
    bottom = jnp.where(last_row, 0.0, gs[1, TH + 1].astype(F32))
    gs[1, 0] = top.astype(BF16)
    gs[1, TH + 1] = bottom.astype(BF16)
    gf[0, 8:40, :] = top
    gf[TH + 1, 8:40, :] = bottom
    gf[:, 7:8, :] = jnp.where(first_col, 0.0, rl[...])
    gf[:, 40:41, :] = jnp.where(last_col, 0.0, rr[...])
    gf[0, 7:8, :] = jnp.where(jnp.logical_or(first_col, first_row), 0.0, rl[0])
    gf[0, 40:41, :] = jnp.where(jnp.logical_or(last_col, first_row), 0.0, rr[0])
    gf[TH + 1, 7:8, :] = jnp.where(jnp.logical_or(first_col, last_row), 0.0, rl[TH + 1])
    gf[TH + 1, 40:41, :] = jnp.where(jnp.logical_or(last_col, last_row), 0.0, rr[TH + 1])

    rows = 8
    chunk = rows * TW

    def first_conv(i, total):
        p = i * rows
        value = (
            dot(ro[pl.ds(p, rows)].reshape(chunk, 3 * CIN), w1[0])
            + dot(re[pl.ds(p, rows)].reshape(chunk, 3 * CIN), w1[1])
            + dot(ro[pl.ds(p + 1, rows)].reshape(chunk, 3 * CIN), w1[2])
        )
        zb[pl.ds(pl.multiple_of(i * chunk, chunk), chunk)] = value
        return total + jnp.sum(value, axis=0, keepdims=True)

    total = lax.fori_loop(0, TH // rows, first_conv, jnp.zeros((1, CMID), F32))
    local_mean = total * (1.0 / PIX)

    def spread(i, total):
        value = zb[pl.ds(pl.multiple_of(i * chunk, chunk), chunk)] - local_mean
        return total + jnp.sum(value * value, axis=0, keepdims=True)

    local_spread = lax.fori_loop(0, TH // rows, spread, jnp.zeros((1, CMID), F32))

    mine_a = y * 2 + core

    def send_core_y(buffer, send_sem, recv_sem):
        return [
            send(buffer.at[mine_a], buffer.at[mine_a], send_sem.at[k], recv_sem.at[k], at_core_y(k))
            for k in range(1, 8)
        ]

    def send_z_hi(buffer, send_sem, recv_sem):
        return [
            send(buffer.at[z_hi], buffer.at[z_hi], send_sem.at[k], recv_sem.at[k], at_z(2 * k))
            for k in range(1, 4)
        ]

    sa[mine_a] = jnp.concatenate([local_mean, local_spread], axis=0)
    stage = send_core_y(sa, sa_send, sa_recv)

    def merged(buffer, count, cells):
        mean = buffer[0, 0:1, :]
        for k in range(1, count):
            mean = mean + buffer[k, 0:1, :]
        mean = mean * (1.0 / count)
        spread_ = jnp.zeros_like(mean)
        for k in range(count):
            shift = buffer[k, 0:1, :] - mean
            spread_ = spread_ + (buffer[k, 1:2, :] + cells * shift * shift)
        return mean, spread_

    def shift_g(p, carry):
        gs[0, p] = gf[p, 9:41, :].astype(BF16)
        gs[2, p] = gf[p, 7:39, :].astype(BF16)
        return carry

    lax.fori_loop(0, TH + 2, shift_g, 0)

    def back_conv(i, carry):
        p = i * rows
        value = jnp.zeros((chunk, CMID), F32)
        for a in range(3):
            for b in range(3):
                window = gs[b, pl.ds(p + 2 - a, rows)].reshape(chunk, CMID)
                value = value + dot_t(window, w2[3 * a + b])
        ab[pl.ds(pl.multiple_of(i * chunk, chunk), chunk)] = value
        return carry

    lax.fori_loop(0, 3, back_conv, 0)
    arrive(stage)
    mean, spread_ = merged(sa, 8, float(PIX))
    sb[z_hi] = jnp.concatenate([mean, spread_], axis=0)
    stage = send_z_hi(sb, sb_send, sb_recv)
    lax.fori_loop(3, 6, back_conv, 0)
    arrive(stage)
    mean, spread_ = merged(sb, 4, float(PIX * 8))
    cells = float(PIX * TILES)
    group_mean = group_sum(mean) * (1.0 / GSIZE)
    shift = mean - group_mean
    group_var = group_sum(spread_ + cells * shift * shift) * (1.0 / (cells * GSIZE))
    inv_std = 1.0 / jnp.sqrt(group_var + 1e-05)
    scale = gain[...]
    offset_ = bias[...]

    def activate(i, sums):
        at = pl.ds(pl.multiple_of(i * chunk, chunk), chunk)
        normed = (zb[at] - group_mean) * inv_std
        shifted = normed * scale + offset_
        gate = 1.0 / (1.0 + jnp.exp(-shifted))
        active = shifted * gate
        pre = ab[at] * gate * (1.0 + shifted * (1.0 - gate))
        zb[at] = normed
        ab[at] = pre
        act_t[:, at] = jnp.transpose(active.astype(BF16))
        one = sums[0] + jnp.sum(pre, axis=0, keepdims=True)
        two = sums[1] + jnp.sum(pre * normed, axis=0, keepdims=True)
        return one, two

    zero = jnp.zeros((1, CMID), F32)
    sum_one, sum_two = lax.fori_loop(0, TH // rows, activate, (zero, zero))
    ta[mine_a] = jnp.concatenate([sum_one, sum_two], axis=0)
    stage = send_core_y(ta, ta_send, ta_recv)

    def second_wgrad(t, carry):
        a, b = t // 3, lax.rem(t, 3)
        window = gs[b, pl.ds(2 - a, TH)].reshape(PIX, CMID)
        value = dot(act_t[...], window)
        at = pl.ds(pl.multiple_of(t * CMID, CMID), CMID)
        p2[0, at] = value[:, 0:128]
        p2[1, at] = value[:, 128:256]
        return carry

    def slot_sum(buffer, count):
        total_ = buffer[0]
        for k in range(1, count):
            total_ = total_ + buffer[k]
        return total_

    lax.fori_loop(0, 4, second_wgrad, 0)
    arrive(stage)
    tb[z_hi] = slot_sum(ta, 8)
    stage = send_z_hi(tb, tb_send, tb_recv)
    lax.fori_loop(4, 9, second_wgrad, 0)

    class Reduce:
        def __init__(self, n, p_, cc, s, rx, q, rz, rc, az, ax, out, ssem, rsem):
            self.n, self.part = n, n // 9
            self.p, self.cc, self.s, self.rx = p_, cc, s, rx
            self.q, self.rz, self.rc, self.az, self.ax = q, rz, rc, az, ax
            self.out, self.ssem, self.rsem = out, ssem, rsem
            self.mine = y * 4 + xx
            self.at = 0

        def sems(self):
            self.at += 1
            return self.ssem.at[self.at - 1], self.rsem.at[self.at - 1]

        def span(self, j):
            return pl.ds(pl.multiple_of(j * self.n, 8), self.n)

        def core_start(self):
            self.flight = [send(self.p.at[1 - core], self.cc, *self.sems(), partner)]

        def core_finish(self):
            arrive(self.flight)

            def body(j, carry):
                value = self.p[core, self.span(j)] + self.cc[self.span(j)]
                self.p[core, self.span(j)] = value
                self.s[j] = value.astype(BF16)
                return carry

            lax.fori_loop(0, 16, body, 0)

        def plane_start(self):
            self.flight = []
            for k in range(1, 16):
                other = lax.rem(y + k // 4, 4) * 4 + lax.rem(xx + k % 4, 4)
                self.flight.append(
                    send(self.s.at[other], self.rx.at[k], *self.sems(), at_plane(k))
                )

        def plane_finish(self):
            arrive(self.flight)
            value = self.p[core, self.span(self.mine)]
            for k in range(1, 16):
                value = value + self.rx[k].astype(F32)
            self.q[...] = value

        def z_start(self):
            part, self.flight = self.part, []
            for k in range(1, 8):
                other = lax.rem(z + k, 8)
                at = pl.ds(pl.multiple_of(other * part, 8), part)
                self.flight.append(
                    send(self.q.at[at], self.rz.at[k], *self.sems(), at_z(k))
                )
                self.flight.append(
                    send(self.q.at[pl.ds(8 * part, part)], self.rc.at[z], *self.sems(), at_z(k))
                )
            self.rc[z] = self.q[pl.ds(8 * part, part)]

        def z_finish(self):
            part = self.part
            arrive(self.flight)
            at = pl.ds(pl.multiple_of(z * part, 8), part)
            value = self.q[at]
            for k in range(1, 8):
                value = value + self.rz[k]
            self.az[at] = value
            self.az[pl.ds(8 * part, part)] = slot_sum(self.rc, 8)

        def z_back_start(self):
            part = self.part
            at = pl.ds(pl.multiple_of(z * part, 8), part)
            self.flight = [
                send(self.az.at[at], self.az.at[at], *self.sems(), at_z(k)) for k in range(1, 8)
            ]

        def z_back_finish(self):
            arrive(self.flight)
            self.ax[core, self.mine] = self.az[...].astype(BF16)

        def plane_back_start(self):
            at = self.ax.at[core, self.mine]
            self.flight = [send(at, at, *self.sems(), at_plane(k)) for k in range(1, 16)]

        def plane_back_finish(self):
            arrive(self.flight)

        def core_back_start(self):
            at = self.ax.at[core]
            self.flight = [send(at, at, *self.sems(), partner)]

        def core_back_finish(self):
            arrive(self.flight)

            def body(j, carry):
                self.out[self.span(j), 0:128] = self.ax[0, j].astype(F32)
                self.out[self.span(j), 128:256] = self.ax[1, j].astype(F32)
                return carry

            lax.fori_loop(0, 16, body, 0)

    second = Reduce(144, p2, cc2, s2, rx2, q2, rz2, rc2, az2, ax2, og2, r2_send, r2_recv)
    first = Reduce(72, p1, cc1, s1, rx1, q1, rz1, rc1, az1, ax1, og1, r1_send, r1_recv)

    second.core_start()
    arrive(stage)
    image_sums = slot_sum(tb, 4)
    n = cells * GSIZE
    mean_shift = group_sum(scale * image_sums[0:1]) * (1.0 / n)
    mean_scale = group_sum(scale * image_sums[1:2]) * (1.0 / n)

    def conv_grad(i, carry):
        at = pl.ds(pl.multiple_of(i * chunk, chunk), chunk)
        value = (scale * ab[at] - mean_shift - zb[at] * mean_scale) * inv_std
        value = value.astype(BF16)
        c0[pl.ds(i * rows, rows)] = value.reshape(rows, TW, CMID)
        cgf[pl.ds(i * rows, rows), 0:TW, :] = value.astype(F32).reshape(rows, TW, CMID)
        act_t[:, at] = jnp.transpose(value)
        return carry

    lax.fori_loop(0, TH // rows, conv_grad, 0)
    cs[...] = cgf[0:TH, 0:1, :]
    error = [
        send(cs, cr.at[pl.ds(0, TH)], c_send.at[0], c_recv.at[0], at_space(-1)),
        send(cs.at[0], cr.at[TH], c_send.at[1], c_recv.at[1], at_space(-5)),
        send(c0.at[0], c0.at[TH], c_send.at[2], c_recv.at[2], at_space(-4)),
    ]
    ux[xx] = image_sums
    share_x = [
        send(ux.at[xx], ux.at[xx], ux_send.at[k], ux_recv.at[k], at_plane(k)) for k in range(1, 4)
    ]

    def first_wgrad(a, window):
        value = jnp.transpose(dot(act_t[...], window.reshape(PIX, 3 * CIN)))
        p1[0, pl.ds(a * 384, 384)] = value[:, 0:128]
        p1[1, pl.ds(a * 384, 384)] = value[:, 128:256]

    first_wgrad(0, ro[0:TH])
    second.core_finish()
    second.plane_start()
    first_wgrad(1, re[...])
    first_wgrad(2, ro[1 : TH + 1])
    first.core_start()

    arrive(error)
    below = jnp.where(last_row, 0.0, c0[TH].astype(F32))
    c0[TH] = below.astype(BF16)
    cgf[TH, 0:TW, :] = below
    cgf[:, TW : TW + 1, :] = jnp.where(last_col, 0.0, cr[...])
    cgf[TH, TW : TW + 1, :] = jnp.where(jnp.logical_or(last_col, last_row), 0.0, cr[TH])

    def shift_c(p, carry):
        c1[p] = cgf[p, 1 : TW + 1, :].astype(BF16)
        return carry

    lax.fori_loop(0, TH + 1, shift_c, 0)
    first.core_finish()
    first.plane_start()

    def up_conv(i, carry):
        p = i * rows
        here = c0[pl.ds(p, rows)].reshape(chunk, CMID)
        down = c0[pl.ds(p + 1, rows)].reshape(chunk, CMID)
        here_right = c1[pl.ds(p, rows)].reshape(chunk, CMID)
        down_right = c1[pl.ds(p + 1, rows)].reshape(chunk, CMID)
        even = dot_t(here, w1[1, 128:384])
        even_odd = even[:, 128:256] + dot_t(here_right, w1[1, 0:128])
        odd = dot_t(here, w1[2, 128:384]) + dot_t(down, w1[0, 128:384])
        odd_odd = odd[:, 128:256] + (
            dot_t(here_right, w1[2, 0:128]) + dot_t(down_right, w1[0, 0:128])
        )
        for parity, left, right in ((0, even[:, 0:128], even_odd), (1, odd[:, 0:128], odd_odd)):
            for r in range(rows):
                slot = 2 * r + parity
                igf[slot, pl.ds(0, TW, stride=2), :] = left[r * TW : (r + 1) * TW]
                igf[slot, pl.ds(1, TW, stride=2), :] = right[r * TW : (r + 1) * TW]
        ig[pl.ds(2 * p, 2 * rows)] = igf[...].astype(BF16)
        return carry

    lax.fori_loop(0, 2, up_conv, 0)
    second.plane_finish()
    second.z_start()
    arrive(share_x)
    uz[z_lo] = slot_sum(ux, 4)
    share_z = [
        send(
            uz.at[z_lo], uz.at[z_lo], uz_send.at[0], uz_recv.at[0],
            at_chip(xx, y, z_hi * 2 + 1 - z_lo, core),
        )
    ]
    lax.fori_loop(2, 4, up_conv, 0)
    first.plane_finish()
    first.z_start()
    second.z_finish()
    second.z_back_start()
    lax.fori_loop(4, 6, up_conv, 0)
    first.z_finish()
    first.z_back_start()
    second.z_back_finish()
    second.plane_back_start()
    first.z_back_finish()
    first.plane_back_start()
    arrive(share_z)
    ogb[...] = slot_sum(uz, 2)
    second.plane_back_finish()
    second.core_back_start()
    first.plane_back_finish()
    first.core_back_start()
    second.core_back_finish()
    first.core_back_finish()
    for copy in pending:
        copy.wait_send()


def on_device(images, first_weight, norm_gain, norm_bias, second_weight, upstream):
    vmem = pltpu.VMEM
    dma = pltpu.SemaphoreType.DMA
    reduce_scratch = []
    for n in (144, 72):
        part = n // 9
        reduce_scratch += [
            vmem((2, 16 * n, 128), F32),
            vmem((16 * n, 128), F32),
            vmem((16, n, 128), BF16),
            vmem((16, n, 128), BF16),
            vmem((n, 128), F32),
            vmem((8, part, 128), F32),
            vmem((8, part, 128), F32),
            vmem((n, 128), F32),
            vmem((2, 16, n, 128), BF16),
        ]
    whole = pl.BlockSpec(memory_space=pltpu.VMEM)
    ig, og1, og2, ogb = pl.pallas_call(
        kernel,
        out_shape=(
            jax.ShapeDtypeStruct((2 * TH, 2 * TW, CIN), BF16),
            jax.ShapeDtypeStruct((9 * CIN, CMID), F32),
            jax.ShapeDtypeStruct((9 * CMID, CMID), F32),
            jax.ShapeDtypeStruct((2, CMID), F32),
        ),
        in_specs=[whole] * 6,
        out_specs=(whole,) * 4,
        scratch_shapes=[
            vmem((2 * TH + 1, 72, CIN), F32),
            vmem((TH, TW, 3 * CIN), BF16),
            vmem((TH + 1, TW, 3 * CIN), BF16),
            vmem((2 * TH, 1, CIN), F32),
            vmem((2 * TH + 1, 1, CIN), F32),
            vmem((2 * TW, CIN), BF16),
            vmem((3, TH + 2, TW, CMID), BF16),
            vmem((TH + 2, 48, CMID), F32),
            vmem((TH, 1, CMID), F32),
            vmem((TH, 1, CMID), F32),
            vmem((TH + 2, 1, CMID), F32),
            vmem((TH + 2, 1, CMID), F32),
            vmem((PIX, CMID), F32),
            vmem((PIX, CMID), F32),
            vmem((CMID, PIX), BF16),
            vmem((TH + 1, 40, CMID), F32),
            vmem((TH + 1, TW, CMID), BF16),
            vmem((TH + 1, TW, CMID), BF16),
            vmem((TH, 1, CMID), F32),
            vmem((TH + 1, 1, CMID), F32),
            vmem((16, 2 * TW, CIN), F32),
            vmem((8, 2, CMID), F32),
            vmem((4, 2, CMID), F32),
            vmem((8, 2, CMID), F32),
            vmem((4, 2, CMID), F32),
            vmem((4, 2, CMID), F32),
            vmem((2, 2, CMID), F32),
            *reduce_scratch,
            dma((11,)), dma((11,)), dma((3,)), dma((3,)),
            dma((8,)), dma((8,)), dma((4,)), dma((4,)),
            dma((8,)), dma((8,)), dma((4,)), dma((4,)),
            dma((4,)), dma((4,)), dma((1,)), dma((1,)),
            dma((53,)), dma((53,)), dma((53,)), dma((53,)),
        ],
        compiler_params=pltpu.CompilerParams(
            collective_id=0, has_side_effects=True, vmem_limit_bytes=62 * 1024 * 1024
        ),
    )(
        images[0, 0],
        first_weight.reshape(3, 3 * CIN, CMID),
        norm_gain.reshape(1, CMID),
        norm_bias.reshape(1, CMID),
        second_weight.reshape(9, CMID, CMID),
        upstream[0, 0],
    )
    return (
        ig[None, None],
        og1.reshape(3, 3, CIN, CMID),
        og2.reshape(3, 3, CMID, CMID),
        ogb[1],
        ogb[0],
    )


def solution(mesh):
    placed = (
        P("dp", "space", None, None, None),
        P(),
        P(),
        P(),
        P(),
        P("dp", "space", None, None, None),
    )
    return jax.shard_map(
        on_device,
        mesh=mesh,
        in_specs=placed,
        out_specs=(P("dp", "space", None, None, None), P(), P(), P(), P()),
        check_vma=False,
    )
```

profile of v0, /device:TPU:1, one launch (start us, length us, event | category | flops | bytes accessed | tf_op | source)
XLA Modules:
  0.0 90.7 jit_solution(4621950716639375553)
XLA Ops:
  0.6 82.5 %shard_map.101 = (bf16[96,64,128]{2,1,0:T(8,128)(2,1)}, f32[1152,256]{1,0:T(8,128)}, f32[2304,256]{1,0:T(8,128)}, f32[2,256]{1,0:T(2,128)}) custom-call(bf16[96,64,128]{2,1,0:T(8,128)(2,1)} %bitcast.12, bf16[3,384,256]{2,1,0:T(8,128)(2,1)} %bitcast.17, f32[1,256]{1,0:T(1,128)} %bitcast.18, f32[1,256]{1,0:T(1,128)} %bitcast.19, ...), custom_call_target="tpu_custom_call" | custom-call | tf_op jit(solution)/shard_map/pallas_call | solution.py:537
  83.1 1.3 %fusion = (f32[1,256]{1,0:T(1,128)}, f32[1,256]{1,0:T(1,128)}) fusion(f32[2,256]{1,0:T(2,128)} %get-tuple-element.12), kind=kLoop, calls=%fused_computation | loop fusion | bytes 4096 | tf_op jit(solution)/shard_map/slice | solution.py:598
  84.5 0.0 copy-start.1
  84.5 2.8 %copy.14 = bf16[1,1,96,64,128]{4,3,2,1,0:T(8,128)(2,1)} copy(bf16[1,1,96,64,128]{4,3,2,1,0:T(8,128)(2,1)} %bitcast.13) | data formatting | bytes 3145728
  87.2 0.0 copy-done.1
  87.2 0.0 copy-start
  87.2 1.0 %copy.15 = f32[3,3,128,256]{3,2,1,0:T(8,128)} copy(f32[3,3,128,256]{3,2,1,0:T(8,128)S(1)} %bitcast.15) | data formatting | bytes 2359296
  88.2 1.1 %copy-done = f32[2304,256]{1,0:T(8,128)S(1)} copy-done((f32[2304,256]{1,0:T(8,128)S(1)}, f32[2304,256]{1,0:T(8,128)}, u32[]{:S(2)}) %copy-start) | copy-done | bytes 2359320
  89.3 1.4 %copy.16 = f32[3,3,256,256]{3,2,1,0:T(8,128)} copy(f32[3,3,256,256]{3,2,1,0:T(8,128)S(1)} %bitcast.11) | data formatting | bytes 4718592
Async XLA Ops:
  84.5 2.8 %copy-start.1 = (f32[1152,256]{1,0:T(8,128)S(1)}, f32[1152,256]{1,0:T(8,128)}, u32[]{:S(2)}) copy-start(f32[1152,256]{1,0:T(8,128)} %get-tuple-element.10) | copy-start | bytes 3538948
  87.2 2.1 %copy-start = (f32[2304,256]{1,0:T(8,128)S(1)}, f32[2304,256]{1,0:T(8,128)}, u32[]{:S(2)}) copy-start(f32[2304,256]{1,0:T(8,128)} %get-tuple-element.11) | copy-start | bytes 7077892
where the time goes:
time: 90.9 us; the launch traced here: 90.7 us
  Pallas kernels  82.5 us (91%)
  local copies, waits for them, and re-layouts  7.58 us (8%)
    pallas_call x1, Pallas kernels, on_device(): pl.pallas_call(kernel, out_shape=(jax.ShapeDtypeStruct((2 * TH, 2 * TW, C...  82.5 us
    unnamed x7, local copies, waits for them, and re-layouts  6.26 us

commit v1 on v0

--- a/solution.py
+++ b/solution.py
@@ -16,7 +16,6 @@
 PIX = TH * TW
 TILES = 32
 GSIZE = 8
-SPACE_OFFSETS = (1, -1, 3, -3, 4, -4, 5, -5)
 
 
 def dot(a, b):
@@ -37,18 +36,18 @@
 
 
 def kernel(
-    x, w1, gain, bias, w2, g,
-    ig, og1, og2, ogb,
-    xf, re, ro, xs, xl, xtop,
+    x_hbm, w1_hbm, gain_hbm, bias_hbm, w2_hbm, g_hbm,
+    ig, ax1, ax2, ogb,
+    x, w1, w2, gain, bias,
+    xe, xf, re, ro, xs, xsc, xl, xlc, xlf, xtop,
     gs, gf, gfirst, glast, rl, rr,
     zb, ab, act_t,
     cgf, c0, c1, cs, cr, igf,
-    sa, sb, ta, tb, ux, uz,
-    p2, cc2, s2, rx2, q2, rz2, rc2, az2, ax2,
-    p1, cc1, s1, rx1, q1, rz1, rc1, az1, ax1,
-    h_send, h_recv, c_send, c_recv,
-    sa_send, sa_recv, sb_send, sb_recv,
-    ta_send, ta_recv, tb_send, tb_recv,
+    sa, ta, ux, uz,
+    p2, cc2, s2, rx2, q2, rz2, rc2, az2,
+    p1, cc1, s1, rx1, q1, rz1, rc1, az1,
+    in_sem, h_send, h_recv, c_send, c_recv,
+    sa_send, sa_recv, ta_send, ta_recv,
     ux_send, ux_recv, uz_send, uz_recv,
     r2_send, r2_recv, r1_send, r1_recv,
 ):
@@ -78,25 +77,38 @@
     def at_z(k):
         return at_chip(xx, y, lax.rem(z + k, 8), core)
 
-    def at_core_y(k):
-        return at_chip(xx, lax.rem(y + k // 2, 4), z, lax.rem(core + k % 2, 2))
-
+    def at_tile(dy, dz, dc):
+        return at_chip(
+            xx, lax.rem(y + dy, 4), lax.rem(z + 2 * dz, 8), lax.rem(core + dc, 2)
+        )
+
+    tiles = [(dy, dz, dc) for dy in (2, 1, 3, 0) for dz in (2, 1, 3, 0) for dc in (1, 0)]
+    tiles = [t for t in tiles if t != (0, 0, 0)]
+    tiles.sort(key=lambda t: -(min(t[0], 4 - t[0]) + 2 * min(t[1], 4 - t[1])))
     partner = at_chip(xx, y, z, 1 - core)
 
     barrier = pltpu.get_barrier_semaphore()
     greeted = 0
-    for offset in SPACE_OFFSETS:
-        pl.semaphore_signal(barrier, inc=1, device_id=at_space(offset), device_id_type=MESH)
+    for device in (
+        [at_tile(*t) for t in tiles]
+        + [at_plane(k) for k in range(1, 16) if k % 4]
+        + [at_z(k) for k in (1, 3, 5, 7)]
+    ):
+        pl.semaphore_signal(barrier, inc=1, device_id=device, device_id_type=MESH)
         greeted += 1
-    for k in range(1, 16):
-        pl.semaphore_signal(barrier, inc=1, device_id=at_plane(k), device_id_type=MESH)
-        greeted += 1
-    for k in range(1, 8):
-        pl.semaphore_signal(barrier, inc=1, device_id=at_z(k), device_id_type=MESH)
-        greeted += 1
-    for k in range(1, 8):
-        pl.semaphore_signal(barrier, inc=1, device_id=at_core_y(k), device_id_type=MESH)
-        greeted += 1
+
+    load_g = pltpu.make_async_copy(g_hbm, gs.at[1, pl.ds(1, TH)], in_sem.at[0])
+    load_x = pltpu.make_async_copy(x_hbm, x, in_sem.at[1])
+    load_w1 = pltpu.make_async_copy(w1_hbm, w1, in_sem.at[2])
+    load_w2 = pltpu.make_async_copy(w2_hbm, w2, in_sem.at[3])
+    load_gain = pltpu.make_async_copy(gain_hbm, gain, in_sem.at[4])
+    load_bias = pltpu.make_async_copy(bias_hbm, bias, in_sem.at[5])
+    load_g.start()
+    load_x.start()
+    load_w1.start()
+    load_w2.start()
+    load_gain.start()
+    load_bias.start()
 
     pending = []
 
@@ -113,23 +125,27 @@
         for copy in copies:
             copy.wait_recv()
 
-    xs[...] = x[:, 48:64, :].astype(F32)[:, 15:16, :]
-
-    def widen_g(p, carry):
-        value = g[p]
-        gs[1, p + 1] = value
-        gf[p + 1, 8:40, :] = value.astype(F32)
-        return carry
-
-    lax.fori_loop(0, TH, widen_g, 0)
+    load_g.wait()
+
+    def widen_g(i, carry):
+        at = pl.ds(1 + 4 * i, 4)
+        gf[at, 8:40, :] = gs[1, at].astype(F32)
+        return carry
+
+    lax.fori_loop(0, TH // 4, widen_g, 0)
     gfirst[...] = gf[1 : TH + 1, 8:9, :]
     glast[...] = gf[1 : TH + 1, 39:40, :]
 
+    load_x.wait()
+    xe[...] = x[:, 56:64, :].astype(F32).reshape(16 * TH, CIN)
+    xs[...] = xe[pl.ds(7, 2 * TH, stride=8), :]
+    xsc[...] = xe[16 * TH - 1 : 16 * TH, :]
+
     pl.semaphore_wait(barrier, greeted)
 
     halo = [
-        send(xs, xl.at[pl.ds(1, 2 * TH)], h_send.at[0], h_recv.at[0], at_space(1)),
-        send(xs.at[2 * TH - 1], xl.at[0], h_send.at[1], h_recv.at[1], at_space(5)),
+        send(xs, xl, h_send.at[0], h_recv.at[0], at_space(1)),
+        send(xsc, xlc, h_send.at[1], h_recv.at[1], at_space(5)),
         send(x.at[2 * TH - 1], xtop, h_send.at[2], h_recv.at[2], at_space(4)),
         send(glast, rl.at[pl.ds(1, TH)], h_send.at[3], h_recv.at[3], at_space(1)),
         send(glast.at[TH - 1], rl.at[0], h_send.at[4], h_recv.at[4], at_space(5)),
@@ -137,36 +153,84 @@
         send(gfirst, rr.at[pl.ds(1, TH)], h_send.at[6], h_recv.at[6], at_space(-1)),
         send(gfirst.at[TH - 1], rr.at[0], h_send.at[7], h_recv.at[7], at_space(3)),
         send(gfirst.at[0], rr.at[TH + 1], h_send.at[8], h_recv.at[8], at_space(-5)),
-        send(g.at[TH - 1], gs.at[1, 0], h_send.at[9], h_recv.at[9], at_space(4)),
-        send(g.at[0], gs.at[1, TH + 1], h_send.at[10], h_recv.at[10], at_space(-4)),
+        send(gs.at[1, TH], gs.at[1, 0], h_send.at[9], h_recv.at[9], at_space(4)),
+        send(gs.at[1, 1], gs.at[1, TH + 1], h_send.at[10], h_recv.at[10], at_space(-4)),
     ]
 
-    def split_x(p, carry):
-        xf[2 * p + 1, 8:72, :] = x[2 * p].astype(F32)
-        xf[2 * p + 2, 8:72, :] = x[2 * p + 1].astype(F32)
-        re[p, :, 128:256] = xf[2 * p + 1, pl.ds(8, TW, stride=2), :].astype(BF16)
-        re[p, :, 256:384] = xf[2 * p + 1, pl.ds(9, TW, stride=2), :].astype(BF16)
-        ro[p + 1, :, 128:256] = xf[2 * p + 2, pl.ds(8, TW, stride=2), :].astype(BF16)
-        ro[p + 1, :, 256:384] = xf[2 * p + 2, pl.ds(9, TW, stride=2), :].astype(BF16)
-        return carry
-
-    lax.fori_loop(0, TH, split_x, 0)
-
-    arrive(halo)
-    xf[0, 8:72, :] = jnp.where(first_row, 0.0, xtop[...].astype(F32))
-    xf[:, 7:8, :] = jnp.where(first_col, 0.0, xl[...])
-    xf[0, 7:8, :] = jnp.where(jnp.logical_or(first_col, first_row), 0.0, xl[0])
-    ro[0, :, 128:256] = xf[0, pl.ds(8, TW, stride=2), :].astype(BF16)
-    ro[0, :, 256:384] = xf[0, pl.ds(9, TW, stride=2), :].astype(BF16)
-
-    def left_x(p, carry):
-        re[p, :, 0:128] = xf[2 * p + 1, pl.ds(7, TW, stride=2), :].astype(BF16)
-        ro[p, :, 0:128] = xf[2 * p, pl.ds(7, TW, stride=2), :].astype(BF16)
-        return carry
-
-    lax.fori_loop(0, TH, left_x, 0)
-    ro[TH, :, 0:128] = xf[2 * TH, pl.ds(7, TW, stride=2), :].astype(BF16)
-
+    xf[pl.ds(7, 2 * TH + 1, stride=72), :] = jnp.zeros((2 * TH + 1, CIN), F32)
+    ro[0] = jnp.zeros((TW, 3 * CIN), BF16)
+
+    def widen_x(i, carry):
+        for r in range(8):
+            at = pl.multiple_of((8 * i + r + 1) * 72 + 8, 8)
+            xf[pl.ds(at, 2 * TW), :] = x[8 * i + r].astype(F32)
+        return carry
+
+    lax.fori_loop(0, TH // 4, widen_x, 0)
+
+    def every_other(block, start):
+        return xf[pl.ds(block * 72 + start, TW, stride=2), :].astype(BF16)
+
+    def split_x(i, carry):
+        for r in range(4):
+            p = 4 * i + r
+            for lane in range(3):
+                at = slice(lane * CIN, (lane + 1) * CIN)
+                re[p, :, at] = every_other(2 * p + 1, 7 + lane)
+                ro[p + 1, :, at] = every_other(2 * p + 2, 7 + lane)
+        return carry
+
+    lax.fori_loop(0, TH // 4, split_x, 0)
+
+    load_w1.wait()
+    rows = 8
+    chunk = rows * TW
+
+    def first_conv(i, total):
+        p = i * rows
+        value = (
+            dot(ro[pl.ds(p, rows)].reshape(chunk, 3 * CIN), w1[0])
+            + dot(re[pl.ds(p, rows)].reshape(chunk, 3 * CIN), w1[1])
+            + dot(ro[pl.ds(p + 1, rows)].reshape(chunk, 3 * CIN), w1[2])
+        )
+        zb[pl.ds(pl.multiple_of(i * chunk, chunk), chunk)] = value
+        return total + jnp.sum(value, axis=0, keepdims=True)
+
+    total = lax.fori_loop(0, TH // rows, first_conv, jnp.zeros((1, CMID), F32))
+
+    arrive(halo[0:3])
+    xlf[0:1, :] = jnp.where(jnp.logical_or(first_col, first_row), 0.0, xlc[...])
+    xlf[1 : 2 * TH + 1, :] = jnp.where(first_col, 0.0, xl[...])
+    xf[8:72, :] = jnp.where(first_row, 0.0, xtop[...].astype(F32))
+    for lane in range(3):
+        ro[0, :, lane * CIN : (lane + 1) * CIN] = every_other(0, 7 + lane)
+    left_rim = jnp.zeros((TH, CMID), F32)
+    for a in range(3):
+        left_rim = left_rim + dot(xlf[pl.ds(a, TH, stride=2), :].astype(BF16), w1[a, 0:CIN])
+    top_rim = dot(ro[0], w1[0])
+    zb[0:TW] += top_rim
+    for p in range(TH):
+        zb[p * TW : p * TW + 1, :] += left_rim[p : p + 1]
+    total = total + jnp.sum(left_rim, axis=0, keepdims=True)
+    total = total + jnp.sum(top_rim, axis=0, keepdims=True)
+    local_mean = total * (1.0 / PIX)
+
+    def spread(i, total):
+        value = zb[pl.ds(pl.multiple_of(i * chunk, chunk), chunk)] - local_mean
+        return total + jnp.sum(value * value, axis=0, keepdims=True)
+
+    local_spread = lax.fori_loop(0, TH // rows, spread, jnp.zeros((1, CMID), F32))
+
+    def share(buffer, send_sem, recv_sem):
+        return [
+            send(buffer.at[sp], buffer.at[sp], send_sem.at[i], recv_sem.at[i], at_tile(*t))
+            for i, t in enumerate(tiles)
+        ]
+
+    sa[sp] = jnp.concatenate([local_mean, local_spread], axis=0)
+    stage = share(sa, sa_send, sa_recv)
+
+    arrive(halo[3:])
     top = jnp.where(first_row, 0.0, gs[1, 0].astype(F32))
     bottom = jnp.where(last_row, 0.0, gs[1, TH + 1].astype(F32))
     gs[1, 0] = top.astype(BF16)
@@ -180,62 +244,13 @@
     gf[TH + 1, 7:8, :] = jnp.where(jnp.logical_or(first_col, last_row), 0.0, rl[TH + 1])
     gf[TH + 1, 40:41, :] = jnp.where(jnp.logical_or(last_col, last_row), 0.0, rr[TH + 1])
 
-    rows = 8
-    chunk = rows * TW
-
-    def first_conv(i, total):
-        p = i * rows
-        value = (
-            dot(ro[pl.ds(p, rows)].reshape(chunk, 3 * CIN), w1[0])
-            + dot(re[pl.ds(p, rows)].reshape(chunk, 3 * CIN), w1[1])
-            + dot(ro[pl.ds(p + 1, rows)].reshape(chunk, 3 * CIN), w1[2])
-        )
-        zb[pl.ds(pl.multiple_of(i * chunk, chunk), chunk)] = value
-        return total + jnp.sum(value, axis=0, keepdims=True)
-
-    total = lax.fori_loop(0, TH // rows, first_conv, jnp.zeros((1, CMID), F32))
-    local_mean = total * (1.0 / PIX)
-
-    def spread(i, total):
-        value = zb[pl.ds(pl.multiple_of(i * chunk, chunk), chunk)] - local_mean
-        return total + jnp.sum(value * value, axis=0, keepdims=True)
-
-    local_spread = lax.fori_loop(0, TH // rows, spread, jnp.zeros((1, CMID), F32))
-
-    mine_a = y * 2 + core
-
-    def send_core_y(buffer, send_sem, recv_sem):
-        return [
-            send(buffer.at[mine_a], buffer.at[mine_a], send_sem.at[k], recv_sem.at[k], at_core_y(k))
-            for k in range(1, 8)
-        ]
-
-    def send_z_hi(buffer, send_sem, recv_sem):
-        return [
-            send(buffer.at[z_hi], buffer.at[z_hi], send_sem.at[k], recv_sem.at[k], at_z(2 * k))
-            for k in range(1, 4)
-        ]
-
-    sa[mine_a] = jnp.concatenate([local_mean, local_spread], axis=0)
-    stage = send_core_y(sa, sa_send, sa_recv)
-
-    def merged(buffer, count, cells):
-        mean = buffer[0, 0:1, :]
-        for k in range(1, count):
-            mean = mean + buffer[k, 0:1, :]
-        mean = mean * (1.0 / count)
-        spread_ = jnp.zeros_like(mean)
-        for k in range(count):
-            shift = buffer[k, 0:1, :] - mean
-            spread_ = spread_ + (buffer[k, 1:2, :] + cells * shift * shift)
-        return mean, spread_
-
-    def shift_g(p, carry):
-        gs[0, p] = gf[p, 9:41, :].astype(BF16)
-        gs[2, p] = gf[p, 7:39, :].astype(BF16)
-        return carry
-
-    lax.fori_loop(0, TH + 2, shift_g, 0)
+    def shift_g(i, carry):
+        at = pl.ds(2 * i, 2)
+        gs[0, at] = gf[at, 9:41, :].astype(BF16)
+        gs[2, at] = gf[at, 7:39, :].astype(BF16)
+        return carry
+
+    lax.fori_loop(0, TH // 2 + 1, shift_g, 0)
 
     def back_conv(i, carry):
         p = i * rows
@@ -247,14 +262,28 @@
         ab[pl.ds(pl.multiple_of(i * chunk, chunk), chunk)] = value
         return carry
 
-    lax.fori_loop(0, 3, back_conv, 0)
+    load_w2.wait()
+    load_gain.wait()
+    load_bias.wait()
+    lax.fori_loop(0, TH // rows, back_conv, 0)
+
+    xf[pl.ds(7, 2 * TH + 1, stride=72), :] = xlf[0 : 2 * TH + 1, :]
+
+    def left_x(i, carry):
+        for r in range(4):
+            p = 4 * i + r
+            re[p, :, 0:CIN] = every_other(2 * p + 1, 7)
+            ro[p, :, 0:CIN] = every_other(2 * p, 7)
+        return carry
+
+    lax.fori_loop(0, TH // 4, left_x, 0)
+    ro[TH, :, 0:CIN] = every_other(2 * TH, 7)
+
     arrive(stage)
-    mean, spread_ = merged(sa, 8, float(PIX))
-    sb[z_hi] = jnp.concatenate([mean, spread_], axis=0)
-    stage = send_z_hi(sb, sb_send, sb_recv)
-    lax.fori_loop(3, 6, back_conv, 0)
-    arrive(stage)
-    mean, spread_ = merged(sb, 4, float(PIX * 8))
+    means, spreads = sa[:, 0:1, :], sa[:, 1:2, :]
+    mean = jnp.sum(means, axis=0) * (1.0 / TILES)
+    shift = means - mean
+    spread_ = jnp.sum(spreads + float(PIX) * (shift * shift), axis=0)
     cells = float(PIX * TILES)
     group_mean = group_sum(mean) * (1.0 / GSIZE)
     shift = mean - group_mean
@@ -279,8 +308,8 @@
 
     zero = jnp.zeros((1, CMID), F32)
     sum_one, sum_two = lax.fori_loop(0, TH // rows, activate, (zero, zero))
-    ta[mine_a] = jnp.concatenate([sum_one, sum_two], axis=0)
-    stage = send_core_y(ta, ta_send, ta_recv)
+    ta[sp] = jnp.concatenate([sum_one, sum_two], axis=0)
+    stage = share(ta, ta_send, ta_recv)
 
     def second_wgrad(t, carry):
         a, b = t // 3, lax.rem(t, 3)
@@ -297,20 +326,15 @@
             total_ = total_ + buffer[k]
         return total_
 
-    lax.fori_loop(0, 4, second_wgrad, 0)
-    arrive(stage)
-    tb[z_hi] = slot_sum(ta, 8)
-    stage = send_z_hi(tb, tb_send, tb_recv)
-    lax.fori_loop(4, 9, second_wgrad, 0)
-
     class Reduce:
-        def __init__(self, n, p_, cc, s, rx, q, rz, rc, az, ax, out, ssem, rsem):
+        def __init__(self, n, p_, cc, s, rx, q, rz, rc, az, ax, ssem, rsem):
             self.n, self.part = n, n // 9
             self.p, self.cc, self.s, self.rx = p_, cc, s, rx
             self.q, self.rz, self.rc, self.az, self.ax = q, rz, rc, az, ax
-            self.out, self.ssem, self.rsem = out, ssem, rsem
+            self.ssem, self.rsem = ssem, rsem
             self.mine = y * 4 + xx
             self.at = 0
+            self.flight = []
 
         def sems(self):
             self.at += 1
@@ -319,8 +343,11 @@
         def span(self, j):
             return pl.ds(pl.multiple_of(j * self.n, 8), self.n)
 
-        def core_start(self):
-            self.flight = [send(self.p.at[1 - core], self.cc, *self.sems(), partner)]
+        def core_start(self, part):
+            size = 16 * self.n // 3
+            at = pl.ds(part * size, size)
+            copy = send(self.p.at[1 - core, at], self.cc.at[at], *self.sems(), partner)
+            self.flight = self.flight + [copy]
 
         def core_finish(self):
             arrive(self.flight)
@@ -385,30 +412,28 @@
         def plane_back_start(self):
             at = self.ax.at[core, self.mine]
             self.flight = [send(at, at, *self.sems(), at_plane(k)) for k in range(1, 16)]
+            self.passed = [send(at, at, *self.sems(), partner)]
 
         def plane_back_finish(self):
-            arrive(self.flight)
-
-        def core_back_start(self):
-            at = self.ax.at[core]
-            self.flight = [send(at, at, *self.sems(), partner)]
+            for k in range(1, 16):
+                arrive([self.flight[k - 1]])
+                owner = lax.rem(y + 4 - k // 4, 4) * 4 + lax.rem(xx + 4 - k % 4, 4)
+                at = self.ax.at[core, owner]
+                self.passed.append(send(at, at, *self.sems(), partner))
 
         def core_back_finish(self):
-            arrive(self.flight)
-
-            def body(j, carry):
-                self.out[self.span(j), 0:128] = self.ax[0, j].astype(F32)
-                self.out[self.span(j), 128:256] = self.ax[1, j].astype(F32)
-                return carry
-
-            lax.fori_loop(0, 16, body, 0)
-
-    second = Reduce(144, p2, cc2, s2, rx2, q2, rz2, rc2, az2, ax2, og2, r2_send, r2_recv)
-    first = Reduce(72, p1, cc1, s1, rx1, q1, rz1, rc1, az1, ax1, og1, r1_send, r1_recv)
-
-    second.core_start()
+            arrive(self.passed)
+
+    second = Reduce(144, p2, cc2, s2, rx2, q2, rz2, rc2, az2, ax2, r2_send, r2_recv)
+    first = Reduce(72, p1, cc1, s1, rx1, q1, rz1, rc1, az1, ax1, r1_send, r1_recv)
+
+    for part in range(3):
+        lax.fori_loop(3 * part, 3 * part + 3, second_wgrad, 0)
+        second.core_start(part)
+    second.core_finish()
+    second.plane_start()
     arrive(stage)
-    image_sums = slot_sum(tb, 4)
+    image_sums = jnp.sum(ta[...], axis=0)
     n = cells * GSIZE
     mean_shift = group_sum(scale * image_sums[0:1]) * (1.0 / n)
     mean_scale = group_sum(scale * image_sums[1:2]) * (1.0 / n)
@@ -440,11 +465,15 @@
         p1[1, pl.ds(a * 384, 384)] = value[:, 128:256]
 
     first_wgrad(0, ro[0:TH])
-    second.core_finish()
-    second.plane_start()
+    first.core_start(0)
     first_wgrad(1, re[...])
+    first.core_start(1)
     first_wgrad(2, ro[1 : TH + 1])
-    first.core_start()
+    first.core_start(2)
+    second.plane_finish()
+    second.z_start()
+    first.core_finish()
+    first.plane_start()
 
     arrive(error)
     below = jnp.where(last_row, 0.0, c0[TH].astype(F32))
@@ -458,8 +487,6 @@
         return carry
 
     lax.fori_loop(0, TH + 1, shift_c, 0)
-    first.core_finish()
-    first.plane_start()
 
     def up_conv(i, carry):
         p = i * rows
@@ -481,9 +508,9 @@
         ig[pl.ds(2 * p, 2 * rows)] = igf[...].astype(BF16)
         return carry
 
-    lax.fori_loop(0, 2, up_conv, 0)
-    second.plane_finish()
-    second.z_start()
+    lax.fori_loop(0, 1, up_conv, 0)
+    second.z_finish()
+    second.z_back_start()
     arrive(share_x)
     uz[z_lo] = slot_sum(ux, 4)
     share_z = [
@@ -492,28 +519,56 @@
             at_chip(xx, y, z_hi * 2 + 1 - z_lo, core),
         )
     ]
-    lax.fori_loop(2, 4, up_conv, 0)
+    lax.fori_loop(1, 3, up_conv, 0)
     first.plane_finish()
     first.z_start()
-    second.z_finish()
-    second.z_back_start()
+    lax.fori_loop(3, 4, up_conv, 0)
+    second.z_back_finish()
+    second.plane_back_start()
     lax.fori_loop(4, 6, up_conv, 0)
+    arrive(share_z)
+    sums = slot_sum(uz, 2)
+    ogb[0] = sums[0:1]
+    ogb[1] = sums[1:2]
     first.z_finish()
     first.z_back_start()
-    second.z_back_finish()
-    second.plane_back_start()
+    second.plane_back_finish()
     first.z_back_finish()
     first.plane_back_start()
-    arrive(share_z)
-    ogb[...] = slot_sum(uz, 2)
-    second.plane_back_finish()
-    second.core_back_start()
+    second.core_back_finish()
     first.plane_back_finish()
-    first.core_back_start()
-    second.core_back_finish()
     first.core_back_finish()
     for copy in pending:
         copy.wait_send()
+
+
+def emit(ig, ax1, ax2, one, out_ig, out1, out2, out_one, out_two, f1, f2, sem):
+    copies = [
+        pltpu.make_async_copy(ig, out_ig, sem.at[0]),
+        pltpu.make_async_copy(one.at[0], out_one, sem.at[1]),
+        pltpu.make_async_copy(one.at[1], out_two, sem.at[2]),
+    ]
+    for copy in copies:
+        copy.start()
+    at = 3
+    for ax, full, out, n, parts in ((ax1, f1, out1, 72, 2), (ax2, f2, out2, 144, 4)):
+        span = 16 // parts
+
+        def widen(j, carry):
+            rows = pl.ds(pl.multiple_of(j * n, 8), n)
+            full[rows, 0:128] = ax[0, j].astype(F32)
+            full[rows, 128:256] = ax[1, j].astype(F32)
+            return carry
+
+        for i in range(parts):
+            lax.fori_loop(i * span, (i + 1) * span, widen, 0)
+            rows = pl.ds(i * span * n, span * n)
+            copy = pltpu.make_async_copy(full.at[rows], out.at[rows], sem.at[at])
+            copy.start()
+            copies.append(copy)
+            at += 1
+    for copy in copies:
+        copy.wait()
 
 
 def on_device(images, first_weight, norm_gain, norm_bias, second_weight, upstream):
@@ -531,25 +586,34 @@
             vmem((8, part, 128), F32),
             vmem((8, part, 128), F32),
             vmem((n, 128), F32),
-            vmem((2, 16, n, 128), BF16),
         ]
     whole = pl.BlockSpec(memory_space=pltpu.VMEM)
-    ig, og1, og2, ogb = pl.pallas_call(
+    outside = pl.BlockSpec(memory_space=pltpu.HBM)
+    results = pl.pallas_call(
         kernel,
         out_shape=(
-            jax.ShapeDtypeStruct((2 * TH, 2 * TW, CIN), BF16),
-            jax.ShapeDtypeStruct((9 * CIN, CMID), F32),
-            jax.ShapeDtypeStruct((9 * CMID, CMID), F32),
-            jax.ShapeDtypeStruct((2, CMID), F32),
+            vmem((2 * TH, 2 * TW, CIN), BF16),
+            vmem((2, 16, 72, 128), BF16),
+            vmem((2, 16, 144, 128), BF16),
+            vmem((2, 1, CMID), F32),
         ),
-        in_specs=[whole] * 6,
+        in_specs=[outside] * 6,
         out_specs=(whole,) * 4,
         scratch_shapes=[
-            vmem((2 * TH + 1, 72, CIN), F32),
+            vmem((2 * TH, 2 * TW, CIN), BF16),
+            vmem((3, 3 * CIN, CMID), BF16),
+            vmem((9, CMID, CMID), BF16),
+            vmem((1, CMID), F32),
+            vmem((1, CMID), F32),
+            vmem((16 * TH, CIN), F32),
+            vmem(((2 * TH + 1) * 72, CIN), F32),
             vmem((TH, TW, 3 * CIN), BF16),
             vmem((TH + 1, TW, 3 * CIN), BF16),
-            vmem((2 * TH, 1, CIN), F32),
-            vmem((2 * TH + 1, 1, CIN), F32),
+            vmem((2 * TH, CIN), F32),
+            vmem((1, CIN), F32),
+            vmem((2 * TH, CIN), F32),
+            vmem((1, CIN), F32),
+            vmem((2 * TH + 8, CIN), F32),
             vmem((2 * TW, CIN), BF16),
             vmem((3, TH + 2, TW, CMID), BF16),
             vmem((TH + 2, 48, CMID), F32),
@@ -566,36 +630,57 @@
             vmem((TH, 1, CMID), F32),
             vmem((TH + 1, 1, CMID), F32),
             vmem((16, 2 * TW, CIN), F32),
-            vmem((8, 2, CMID), F32),
-            vmem((4, 2, CMID), F32),
-            vmem((8, 2, CMID), F32),
-            vmem((4, 2, CMID), F32),
+            vmem((TILES, 2, CMID), F32),
+            vmem((TILES, 2, CMID), F32),
             vmem((4, 2, CMID), F32),
             vmem((2, 2, CMID), F32),
             *reduce_scratch,
-            dma((11,)), dma((11,)), dma((3,)), dma((3,)),
-            dma((8,)), dma((8,)), dma((4,)), dma((4,)),
-            dma((8,)), dma((8,)), dma((4,)), dma((4,)),
+            dma((6,)), dma((11,)), dma((11,)), dma((3,)), dma((3,)),
+            dma((31,)), dma((31,)), dma((31,)), dma((31,)),
             dma((4,)), dma((4,)), dma((1,)), dma((1,)),
-            dma((53,)), dma((53,)), dma((53,)), dma((53,)),
+            dma((70,)), dma((70,)), dma((70,)), dma((70,)),
         ],
         compiler_params=pltpu.CompilerParams(
-            collective_id=0, has_side_effects=True, vmem_limit_bytes=62 * 1024 * 1024
+            collective_id=0, has_side_effects=True, vmem_limit_bytes=50 * 1024 * 1024
         ),
     )(
-        images[0, 0],
-        first_weight.reshape(3, 3 * CIN, CMID),
-        norm_gain.reshape(1, CMID),
-        norm_bias.reshape(1, CMID),
-        second_weight.reshape(9, CMID, CMID),
-        upstream[0, 0],
+        *[
+            pltpu.with_memory_space_constraint(r, pltpu.HBM)
+            for r in (
+                images[0, 0],
+                first_weight.reshape(3, 3 * CIN, CMID),
+                norm_gain.reshape(1, CMID),
+                norm_bias.reshape(1, CMID),
+                second_weight.reshape(9, CMID, CMID),
+                upstream[0, 0],
+            )
+        ]
     )
+    inside = [pltpu.with_memory_space_constraint(r, pltpu.VMEM) for r in results]
+    ig, og1, og2, one, two = pl.pallas_call(
+        emit,
+        out_shape=(
+            jax.ShapeDtypeStruct((2 * TH, 2 * TW, CIN), BF16),
+            jax.ShapeDtypeStruct((9 * CIN, CMID), F32),
+            jax.ShapeDtypeStruct((9 * CMID, CMID), F32),
+            jax.ShapeDtypeStruct((1, CMID), F32),
+            jax.ShapeDtypeStruct((1, CMID), F32),
+        ),
+        in_specs=[whole] * 4,
+        out_specs=(outside,) * 5,
+        scratch_shapes=[
+            vmem((9 * CIN, CMID), F32),
+            vmem((9 * CMID, CMID), F32),
+            dma((9,)),
+        ],
+        compiler_params=pltpu.CompilerParams(vmem_limit_bytes=8 * 1024 * 1024),
+    )(*inside)
     return (
         ig[None, None],
         og1.reshape(3, 3, CIN, CMID),
         og2.reshape(3, 3, CMID, CMID),
-        ogb[1],
-        ogb[0],
+        two[0],
+        one[0],
     )
 
 

time: 90.9 us -> 77.2 us (0.85)
  local copies, waits for them, and re-layouts: 7.58 us -> 0 us
  Pallas kernels: 82.5 us -> 76.5 us
    unnamed x7 -> x0, local copies, waits for them, and re-layouts: 6.26 us -> none
    pallas_call x1 -> x2, Pallas kernels: 82.5 us -> 76.5 us  [the longest x1 74.1 us: on_device(): pl.pallas_call(kernel, out_shape=(vmem((2 * TH, 2 * TW, CIN), BF16), vmem...]
    slice x1 -> x0, local copies, waits for them, and re-layouts: 1.32 us -> none  [on_device(): ogb[0]]
where the time goes in v1:
time: 77.2 us; the launch traced here: 77.1 us
  Pallas kernels  76.5 us (99%)
    pallas_call x1, Pallas kernels, on_device(): pl.pallas_call(kernel, out_shape=(vmem((2 * TH, 2 * TW, CIN), BF16), vmem...  74.1 us
    pallas_call x1, Pallas kernels, on_device(): pl.pallas_call(emit, out_shape=(jax.ShapeDtypeStruct((2 * TH, 2 * TW, CIN...  2.39 us

profile of v1, /device:TPU:1, one launch (start us, length us, event | category | flops | bytes accessed | tf_op | source)
XLA Modules:
  0.0 77.1 jit_solution(17296986926645860150)
XLA Ops:
  0.6 74.1 %shard_map.101 = (bf16[96,64,128]{2,1,0:T(8,128)(2,1)S(1)}, bf16[2,16,72,128]{3,2,1,0:T(8,128)(2,1)S(1)}, bf16[2,16,144,128]{3,2,1,0:T(8,128)(2,1)S(1)}, f32[2,1,256]{2,1,0:T(1,128)S(1)}) custom-call(bf16[96,64,128]{2,1,0:T(8,128)(2,1)} %bitcast.11, bf16[3,384,256]{2,1,0:T(8,128)(2,1)} %bitcast.14, f32[1,256]{1,0:T(1,128)} %bitcast.15, f32[1,256]{1,0:T(1,128)} %bitcast.16, ...), custom_call_target="tpu_custom_call" | custom-call | tf_op jit(solution)/shard_map/pallas_call | solution.py:592
  74.7 2.4 %shard_map.102 = (bf16[96,64,128]{2,1,0:T(8,128)(2,1)}, f32[1152,256]{1,0:T(8,128)}, f32[2304,256]{1,0:T(8,128)}, f32[1,256]{1,0:T(1,128)}, f32[1,256]{1,0:T(1,128)}) custom-call(bf16[96,64,128]{2,1,0:T(8,128)(2,1)S(1)} %get-tuple-element.14.ig, bf16[2,16,72,128]{3,2,1,0:T(8,128)(2,1)S(1)} %get-tuple-element.15.ax1, ...), custom_call_target="tpu_custom_call" | custom-call | tf_op jit(solution)/shard_map/pallas_call | solution.py:660

commit v2 on v1

--- a/solution.py
+++ b/solution.py
@@ -16,6 +16,9 @@
 PIX = TH * TW
 TILES = 32
 GSIZE = 8
+PIECE = 72
+PLANE = (10, 9, 11, 6, 14, 2, 8, 5, 7, 13, 15, 1, 3, 4, 12)
+ZS = (4, 3, 5, 2, 6, 1, 7)
 
 
 def dot(a, b):
@@ -37,19 +40,20 @@
 
 def kernel(
     x_hbm, w1_hbm, gain_hbm, bias_hbm, w2_hbm, g_hbm,
-    ig, ax1, ax2, ogb,
+    ig, axf, axa, axb, ogb,
     x, w1, w2, gain, bias,
     xe, xf, re, ro, xs, xsc, xl, xlc, xlf, xtop,
     gs, gf, gfirst, glast, rl, rr,
-    zb, ab, act_t,
+    zb, ab, act, act_t, xt,
     cgf, c0, c1, cs, cr, igf,
     sa, ta, ux, uz,
-    p2, cc2, s2, rx2, q2, rz2, rc2, az2,
-    p1, cc1, s1, rx1, q1, rz1, rc1, az1,
+    pa, ca, sta, rxa, qa, rza, aza,
+    pb, cb, stb, rxb, qb, rzb, azb,
+    pf, cf, stf, rxf, qf, rzf, azf,
     in_sem, h_send, h_recv, c_send, c_recv,
     sa_send, sa_recv, ta_send, ta_recv,
     ux_send, ux_recv, uz_send, uz_recv,
-    r2_send, r2_recv, r1_send, r1_recv,
+    ra_send, ra_recv, rb_send, rb_recv, rf_send, rf_recv,
 ):
     dp = lax.axis_index("dp")
     sp = lax.axis_index("space")
@@ -87,16 +91,6 @@
     tiles.sort(key=lambda t: -(min(t[0], 4 - t[0]) + 2 * min(t[1], 4 - t[1])))
     partner = at_chip(xx, y, z, 1 - core)
 
-    barrier = pltpu.get_barrier_semaphore()
-    greeted = 0
-    for device in (
-        [at_tile(*t) for t in tiles]
-        + [at_plane(k) for k in range(1, 16) if k % 4]
-        + [at_z(k) for k in (1, 3, 5, 7)]
-    ):
-        pl.semaphore_signal(barrier, inc=1, device_id=device, device_id_type=MESH)
-        greeted += 1
-
     load_g = pltpu.make_async_copy(g_hbm, gs.at[1, pl.ds(1, TH)], in_sem.at[0])
     load_x = pltpu.make_async_copy(x_hbm, x, in_sem.at[1])
     load_w1 = pltpu.make_async_copy(w1_hbm, w1, in_sem.at[2])
@@ -109,6 +103,16 @@
     load_w2.start()
     load_gain.start()
     load_bias.start()
+
+    barrier = pltpu.get_barrier_semaphore()
+    greeted = 0
+    for device in (
+        [at_tile(*t) for t in tiles]
+        + [at_plane(k) for k in (10, 9, 11, 6, 14, 2, 5, 7, 13, 15, 1, 3)]
+        + [at_z(k) for k in (1, 3, 5, 7)]
+    ):
+        pl.semaphore_signal(barrier, inc=1, device_id=device, device_id_type=MESH)
+        greeted += 1
 
     pending = []
 
@@ -279,6 +283,16 @@
     lax.fori_loop(0, TH // 4, left_x, 0)
     ro[TH, :, 0:CIN] = every_other(2 * TH, 7)
 
+    def turn_x(i, carry):
+        at = pl.ds(pl.multiple_of(i * chunk, chunk), chunk)
+        p = i * rows
+        xt[0, :, at] = jnp.transpose(ro[pl.ds(p, rows)].reshape(chunk, 3 * CIN))
+        xt[1, :, at] = jnp.transpose(re[pl.ds(p, rows)].reshape(chunk, 3 * CIN))
+        xt[2, :, at] = jnp.transpose(ro[pl.ds(p + 1, rows)].reshape(chunk, 3 * CIN))
+        return carry
+
+    lax.fori_loop(0, TH // rows, turn_x, 0)
+
     arrive(stage)
     means, spreads = sa[:, 0:1, :], sa[:, 1:2, :]
     mean = jnp.sum(means, axis=0) * (1.0 / TILES)
@@ -301,7 +315,7 @@
         pre = ab[at] * gate * (1.0 + shifted * (1.0 - gate))
         zb[at] = normed
         ab[at] = pre
-        act_t[:, at] = jnp.transpose(active.astype(BF16))
+        act[at] = active.astype(BF16)
         one = sums[0] + jnp.sum(pre, axis=0, keepdims=True)
         two = sums[1] + jnp.sum(pre * normed, axis=0, keepdims=True)
         return one, two
@@ -311,13 +325,27 @@
     ta[sp] = jnp.concatenate([sum_one, sum_two], axis=0)
     stage = share(ta, ta_send, ta_recv)
 
-    def second_wgrad(t, carry):
-        a, b = t // 3, lax.rem(t, 3)
-        window = gs[b, pl.ds(2 - a, TH)].reshape(PIX, CMID)
-        value = dot(act_t[...], window)
-        at = pl.ds(pl.multiple_of(t * CMID, CMID), CMID)
-        p2[0, at] = value[:, 0:128]
-        p2[1, at] = value[:, 128:256]
+    def turn(i, carry):
+        at = pl.ds(pl.multiple_of(i * chunk, chunk), chunk)
+        act_t[:, at] = jnp.transpose(act[at])
+        return carry
+
+    lax.fori_loop(0, TH // rows, turn, 0)
+
+    def second_tap(t):
+        window = gs[lax.rem(t, 3), pl.ds(2 - t // 3, TH)].reshape(PIX, CMID)
+        return dot(act_t[...], window)
+
+    def put(target, at, value):
+        target[0, at] = value[:, 0:128]
+        target[1, at] = value[:, 128:256]
+
+    def second_a(t, carry):
+        put(pa, pl.ds(pl.multiple_of(t * CMID, CMID), CMID), second_tap(t))
+        return carry
+
+    def second_b(t, carry):
+        put(pb, pl.ds(pl.multiple_of(t * CMID - 9 * 128, 128), CMID), second_tap(t))
         return carry
 
     def slot_sum(buffer, count):
@@ -327,10 +355,9 @@
         return total_
 
     class Reduce:
-        def __init__(self, n, p_, cc, s, rx, q, rz, rc, az, ax, ssem, rsem):
-            self.n, self.part = n, n // 9
+        def __init__(self, p_, cc, s, rx, q, rz, az, ax, ssem, rsem):
             self.p, self.cc, self.s, self.rx = p_, cc, s, rx
-            self.q, self.rz, self.rc, self.az, self.ax = q, rz, rc, az, ax
+            self.q, self.rz, self.az, self.ax = q, rz, az, ax
             self.ssem, self.rsem = ssem, rsem
             self.mine = y * 4 + xx
             self.at = 0
@@ -341,11 +368,10 @@
             return self.ssem.at[self.at - 1], self.rsem.at[self.at - 1]
 
         def span(self, j):
-            return pl.ds(pl.multiple_of(j * self.n, 8), self.n)
-
-        def core_start(self, part):
-            size = 16 * self.n // 3
-            at = pl.ds(part * size, size)
+            return pl.ds(pl.multiple_of(j * PIECE, 8), PIECE)
+
+        def core_start(self, low, high):
+            at = pl.ds(low, high - low)
             copy = send(self.p.at[1 - core, at], self.cc.at[at], *self.sems(), partner)
             self.flight = self.flight + [copy]
 
@@ -362,7 +388,7 @@
 
         def plane_start(self):
             self.flight = []
-            for k in range(1, 16):
+            for k in PLANE:
                 other = lax.rem(y + k // 4, 4) * 4 + lax.rem(xx + k % 4, 4)
                 self.flight.append(
                     send(self.s.at[other], self.rx.at[k], *self.sems(), at_plane(k))
@@ -373,50 +399,39 @@
             value = self.p[core, self.span(self.mine)]
             for k in range(1, 16):
                 value = value + self.rx[k].astype(F32)
-            self.q[...] = value
+            for k in range(8):
+                self.q[k] = value[9 * k : 9 * k + 9]
 
         def z_start(self):
-            part, self.flight = self.part, []
-            for k in range(1, 8):
-                other = lax.rem(z + k, 8)
-                at = pl.ds(pl.multiple_of(other * part, 8), part)
-                self.flight.append(
-                    send(self.q.at[at], self.rz.at[k], *self.sems(), at_z(k))
-                )
-                self.flight.append(
-                    send(self.q.at[pl.ds(8 * part, part)], self.rc.at[z], *self.sems(), at_z(k))
-                )
-            self.rc[z] = self.q[pl.ds(8 * part, part)]
+            self.flight = [
+                send(self.q.at[lax.rem(z + k, 8)], self.rz.at[k], *self.sems(), at_z(k))
+                for k in ZS
+            ]
 
         def z_finish(self):
-            part = self.part
             arrive(self.flight)
-            at = pl.ds(pl.multiple_of(z * part, 8), part)
-            value = self.q[at]
+            value = self.q[z]
             for k in range(1, 8):
                 value = value + self.rz[k]
-            self.az[at] = value
-            self.az[pl.ds(8 * part, part)] = slot_sum(self.rc, 8)
+            self.az[z] = value
 
         def z_back_start(self):
-            part = self.part
-            at = pl.ds(pl.multiple_of(z * part, 8), part)
-            self.flight = [
-                send(self.az.at[at], self.az.at[at], *self.sems(), at_z(k)) for k in range(1, 8)
-            ]
+            at = self.az.at[z]
+            self.flight = [send(at, at, *self.sems(), at_z(k)) for k in ZS]
 
         def z_back_finish(self):
             arrive(self.flight)
-            self.ax[core, self.mine] = self.az[...].astype(BF16)
+            value = jnp.concatenate([self.az[k] for k in range(8)], axis=0)
+            self.ax[core, self.mine] = value.astype(BF16)
 
         def plane_back_start(self):
             at = self.ax.at[core, self.mine]
-            self.flight = [send(at, at, *self.sems(), at_plane(k)) for k in range(1, 16)]
+            self.flight = [(k, send(at, at, *self.sems(), at_plane(k))) for k in PLANE]
             self.passed = [send(at, at, *self.sems(), partner)]
 
         def plane_back_finish(self):
-            for k in range(1, 16):
-                arrive([self.flight[k - 1]])
+            for k, copy in reversed(self.flight):
+                arrive([copy])
                 owner = lax.rem(y + 4 - k // 4, 4) * 4 + lax.rem(xx + 4 - k % 4, 4)
                 at = self.ax.at[core, owner]
                 self.passed.append(send(at, at, *self.sems(), partner))
@@ -424,14 +439,25 @@
         def core_back_finish(self):
             arrive(self.passed)
 
-    second = Reduce(144, p2, cc2, s2, rx2, q2, rz2, rc2, az2, ax2, r2_send, r2_recv)
-    first = Reduce(72, p1, cc1, s1, rx1, q1, rz1, rc1, az1, ax1, r1_send, r1_recv)
-
-    for part in range(3):
-        lax.fori_loop(3 * part, 3 * part + 3, second_wgrad, 0)
-        second.core_start(part)
-    second.core_finish()
-    second.plane_start()
+    one = Reduce(pa, ca, sta, rxa, qa, rza, aza, axa, ra_send, ra_recv)
+    two = Reduce(pb, cb, stb, rxb, qb, rzb, azb, axb, rb_send, rb_recv)
+    three = Reduce(pf, cf, stf, rxf, qf, rzf, azf, axf, rf_send, rf_recv)
+
+    lax.fori_loop(0, 2, second_a, 0)
+    one.core_start(0, 512)
+    lax.fori_loop(2, 4, second_a, 0)
+    middle = second_tap(jnp.int32(4))
+    put(pa, pl.ds(1024, 128), middle[0:128])
+    put(pb, pl.ds(0, 128), middle[128:256])
+    one.core_start(512, 1152)
+    lax.fori_loop(5, 7, second_b, 0)
+    two.core_start(0, 640)
+    one.core_finish()
+    one.plane_start()
+    lax.fori_loop(7, 9, second_b, 0)
+    two.core_start(640, 1152)
+    two.core_finish()
+    two.plane_start()
     arrive(stage)
     image_sums = jnp.sum(ta[...], axis=0)
     n = cells * GSIZE
@@ -444,7 +470,6 @@
         value = value.astype(BF16)
         c0[pl.ds(i * rows, rows)] = value.reshape(rows, TW, CMID)
         cgf[pl.ds(i * rows, rows), 0:TW, :] = value.astype(F32).reshape(rows, TW, CMID)
-        act_t[:, at] = jnp.transpose(value)
         return carry
 
     lax.fori_loop(0, TH // rows, conv_grad, 0)
@@ -459,21 +484,13 @@
         send(ux.at[xx], ux.at[xx], ux_send.at[k], ux_recv.at[k], at_plane(k)) for k in range(1, 4)
     ]
 
-    def first_wgrad(a, window):
-        value = jnp.transpose(dot(act_t[...], window.reshape(PIX, 3 * CIN)))
-        p1[0, pl.ds(a * 384, 384)] = value[:, 0:128]
-        p1[1, pl.ds(a * 384, 384)] = value[:, 128:256]
-
-    first_wgrad(0, ro[0:TH])
-    first.core_start(0)
-    first_wgrad(1, re[...])
-    first.core_start(1)
-    first_wgrad(2, ro[1 : TH + 1])
-    first.core_start(2)
-    second.plane_finish()
-    second.z_start()
-    first.core_finish()
-    first.plane_start()
+    def first_wgrad(a):
+        value = dot(xt[a], c0[0:TH].reshape(PIX, CMID))
+        put(pf, pl.ds(a * 384, 384), value)
+
+    for a in range(3):
+        first_wgrad(a)
+        three.core_start(a * 384, a * 384 + 384)
 
     arrive(error)
     below = jnp.where(last_row, 0.0, c0[TH].astype(F32))
@@ -482,11 +499,12 @@
     cgf[:, TW : TW + 1, :] = jnp.where(last_col, 0.0, cr[...])
     cgf[TH, TW : TW + 1, :] = jnp.where(jnp.logical_or(last_col, last_row), 0.0, cr[TH])
 
-    def shift_c(p, carry):
-        c1[p] = cgf[p, 1 : TW + 1, :].astype(BF16)
-        return carry
-
-    lax.fori_loop(0, TH + 1, shift_c, 0)
+    def shift_c(i, carry):
+        at = pl.ds(7 * i, 7)
+        c1[at] = cgf[at, 1 : TW + 1, :].astype(BF16)
+        return carry
+
+    lax.fori_loop(0, (TH + 1) // 7, shift_c, 0)
 
     def up_conv(i, carry):
         p = i * rows
@@ -508,9 +526,10 @@
         ig[pl.ds(2 * p, 2 * rows)] = igf[...].astype(BF16)
         return carry
 
-    lax.fori_loop(0, 1, up_conv, 0)
-    second.z_finish()
-    second.z_back_start()
+    three.core_finish()
+    three.plane_start()
+    one.plane_finish()
+    one.z_start()
     arrive(share_x)
     uz[z_lo] = slot_sum(ux, 4)
     share_z = [
@@ -519,30 +538,44 @@
             at_chip(xx, y, z_hi * 2 + 1 - z_lo, core),
         )
     ]
+    lax.fori_loop(0, 1, up_conv, 0)
+    two.plane_finish()
+    two.z_start()
     lax.fori_loop(1, 3, up_conv, 0)
-    first.plane_finish()
-    first.z_start()
-    lax.fori_loop(3, 4, up_conv, 0)
-    second.z_back_finish()
-    second.plane_back_start()
-    lax.fori_loop(4, 6, up_conv, 0)
+    one.z_finish()
+    one.z_back_start()
+    three.plane_finish()
+    three.z_start()
+    lax.fori_loop(3, 5, up_conv, 0)
+    two.z_finish()
+    two.z_back_start()
+    one.z_back_finish()
+    one.plane_back_start()
+    three.z_finish()
+    three.z_back_start()
+    two.z_back_finish()
+    two.plane_back_start()
+    lax.fori_loop(5, 6, up_conv, 0)
     arrive(share_z)
     sums = slot_sum(uz, 2)
     ogb[0] = sums[0:1]
     ogb[1] = sums[1:2]
-    first.z_finish()
-    first.z_back_start()
-    second.plane_back_finish()
-    first.z_back_finish()
-    first.plane_back_start()
-    second.core_back_finish()
-    first.plane_back_finish()
-    first.core_back_finish()
-    for copy in pending:
+    one.plane_back_finish()
+    three.z_back_finish()
+    three.plane_back_start()
+    drained = len(pending) - 16
+    two.plane_back_finish()
+    one.core_back_finish()
+    for copy in pending[:drained]:
         copy.wait_send()
-
-
-def emit(ig, ax1, ax2, one, out_ig, out1, out2, out_one, out_two, f1, f2, sem):
+    three.plane_back_finish()
+    two.core_back_finish()
+    three.core_back_finish()
+    for copy in pending[drained:]:
+        copy.wait_send()
+
+
+def emit(ig, axf, axa, axb, one, out_ig, out1, out2, out_one, out_two, f1, f2, sem):
     copies = [
         pltpu.make_async_copy(ig, out_ig, sem.at[0]),
         pltpu.make_async_copy(one.at[0], out_one, sem.at[1]),
@@ -551,18 +584,17 @@
     for copy in copies:
         copy.start()
     at = 3
-    for ax, full, out, n, parts in ((ax1, f1, out1, 72, 2), (ax2, f2, out2, 144, 4)):
-        span = 16 // parts
+    for ax, full, out, base in ((axa, f2, out2, 0), (axb, f2, out2, 16), (axf, f1, out1, 0)):
 
         def widen(j, carry):
-            rows = pl.ds(pl.multiple_of(j * n, 8), n)
+            rows = pl.ds(pl.multiple_of((base + j) * PIECE, 8), PIECE)
             full[rows, 0:128] = ax[0, j].astype(F32)
             full[rows, 128:256] = ax[1, j].astype(F32)
             return carry
 
-        for i in range(parts):
-            lax.fori_loop(i * span, (i + 1) * span, widen, 0)
-            rows = pl.ds(i * span * n, span * n)
+        for half in range(2):
+            lax.fori_loop(8 * half, 8 * half + 8, widen, 0)
+            rows = pl.ds((base + 8 * half) * PIECE, 8 * PIECE)
             copy = pltpu.make_async_copy(full.at[rows], out.at[rows], sem.at[at])
             copy.start()
             copies.append(copy)
@@ -574,31 +606,28 @@
 def on_device(images, first_weight, norm_gain, norm_bias, second_weight, upstream):
     vmem = pltpu.VMEM
     dma = pltpu.SemaphoreType.DMA
-    reduce_scratch = []
-    for n in (144, 72):
-        part = n // 9
-        reduce_scratch += [
-            vmem((2, 16 * n, 128), F32),
-            vmem((16 * n, 128), F32),
-            vmem((16, n, 128), BF16),
-            vmem((16, n, 128), BF16),
-            vmem((n, 128), F32),
-            vmem((8, part, 128), F32),
-            vmem((8, part, 128), F32),
-            vmem((n, 128), F32),
-        ]
+    reduce_scratch = [
+        vmem((2, 16 * PIECE, 128), F32),
+        vmem((16 * PIECE, 128), F32),
+        vmem((16, PIECE, 128), BF16),
+        vmem((16, PIECE, 128), BF16),
+        vmem((8, 9, 128), F32),
+        vmem((8, 9, 128), F32),
+        vmem((8, 9, 128), F32),
+    ] * 3
     whole = pl.BlockSpec(memory_space=pltpu.VMEM)
     outside = pl.BlockSpec(memory_space=pltpu.HBM)
     results = pl.pallas_call(
         kernel,
         out_shape=(
             vmem((2 * TH, 2 * TW, CIN), BF16),
-            vmem((2, 16, 72, 128), BF16),
-            vmem((2, 16, 144, 128), BF16),
+            vmem((2, 16, PIECE, 128), BF16),
+            vmem((2, 16, PIECE, 128), BF16),
+            vmem((2, 16, PIECE, 128), BF16),
             vmem((2, 1, CMID), F32),
         ),
         in_specs=[outside] * 6,
-        out_specs=(whole,) * 4,
+        out_specs=(whole,) * 5,
         scratch_shapes=[
             vmem((2 * TH, 2 * TW, CIN), BF16),
             vmem((3, 3 * CIN, CMID), BF16),
@@ -623,7 +652,9 @@
             vmem((TH + 2, 1, CMID), F32),
             vmem((PIX, CMID), F32),
             vmem((PIX, CMID), F32),
+            vmem((PIX, CMID), BF16),
             vmem((CMID, PIX), BF16),
+            vmem((3, 3 * CIN, PIX), BF16),
             vmem((TH + 1, 40, CMID), F32),
             vmem((TH + 1, TW, CMID), BF16),
             vmem((TH + 1, TW, CMID), BF16),
@@ -638,7 +669,7 @@
             dma((6,)), dma((11,)), dma((11,)), dma((3,)), dma((3,)),
             dma((31,)), dma((31,)), dma((31,)), dma((31,)),
             dma((4,)), dma((4,)), dma((1,)), dma((1,)),
-            dma((70,)), dma((70,)), dma((70,)), dma((70,)),
+            dma((63,)), dma((63,)), dma((63,)), dma((63,)), dma((63,)), dma((63,)),
         ],
         compiler_params=pltpu.CompilerParams(
             collective_id=0, has_side_effects=True, vmem_limit_bytes=50 * 1024 * 1024
@@ -666,7 +697,7 @@
             jax.ShapeDtypeStruct((1, CMID), F32),
             jax.ShapeDtypeStruct((1, CMID), F32),
         ),
-        in_specs=[whole] * 4,
+        in_specs=[whole] * 5,
         out_specs=(outside,) * 5,
         scratch_shapes=[
             vmem((9 * CIN, CMID), F32),

time: 77.2 us -> 71.4 us (0.925)
  Pallas kernels: 76.5 us -> 70.7 us
    pallas_call x1, Pallas kernels: 74.1 us -> 68.3 us  [on_device(): pl.pallas_call(kernel, out_shape=(vmem((2 * TH, 2 * TW, CIN), BF16), vmem...]
where the time goes in v2:
time: 71.4 us
  Pallas kernels  70.7 us (99%)
    pallas_call x1, Pallas kernels, on_device(): pl.pallas_call(kernel, out_shape=(vmem((2 * TH, 2 * TW, CIN), BF16), vmem...  68.3 us
    pallas_call x1, Pallas kernels, on_device(): pl.pallas_call(emit, out_shape=(jax.ShapeDtypeStruct((2 * TH, 2 * TW, CIN...  2.39 us

profile of v2, /device:TPU:1, one launch (start us, length us, event | category | flops | bytes accessed | tf_op | source)
XLA Modules:
  0.0 71.4 jit_solution(12645906148577159912)
XLA Ops:
  0.6 68.3 %shard_map.101 = (bf16[96,64,128]{2,1,0:T(8,128)(2,1)S(1)}, bf16[2,16,72,128]{3,2,1,0:T(8,128)(2,1)S(1)}, bf16[2,16,72,128]{3,2,1,0:T(8,128)(2,1)S(1)}, bf16[2,1...) custom-call(bf16[96,64,128]{2,1,0:T(8,128)(2,1)} %bitcast.11, bf16[3,384,256]{2,1,0:T(8,128)(2,1)} %bitcast.14, ...), custom_call_target="tpu_custom_call" | custom-call | tf_op jit(solution)/shard_map/pallas_call | solution.py:620
  69.0 2.4 %shard_map.102 = (bf16[96,64,128]{2,1,0:T(8,128)(2,1)}, f32[1152,256]{1,0:T(8,128)}, f32[2304,256]{1,0:T(8,128)}, f32[1,256]{1,0:T(1,128)}, f32[1,256]{1,0:T(1,128)}) custom-call(bf16[96,64,128]{2,1,0:T(8,128)(2,1)S(1)} %get-tuple-element.15.ig, bf16[2,16,72,128]{3,2,1,0:T(8,128)(2,1)S(1)} %get-tuple-element.16.axf, ...), custom_call_target="tpu_custom_call" | custom-call | tf_op jit(solution)/shard_map/pallas_call | solution.py:691

commit v3 on v2

--- a/solution.py
+++ b/solution.py
@@ -249,12 +249,12 @@
     gf[TH + 1, 40:41, :] = jnp.where(jnp.logical_or(last_col, last_row), 0.0, rr[TH + 1])
 
     def shift_g(i, carry):
-        at = pl.ds(2 * i, 2)
+        at = pl.ds(5 * i, 5)
         gs[0, at] = gf[at, 9:41, :].astype(BF16)
         gs[2, at] = gf[at, 7:39, :].astype(BF16)
         return carry
 
-    lax.fori_loop(0, TH // 2 + 1, shift_g, 0)
+    lax.fori_loop(0, (TH + 2) // 5, shift_g, 0)
 
     def back_conv(i, carry):
         p = i * rows
@@ -306,22 +306,25 @@
     scale = gain[...]
     offset_ = bias[...]
 
+    slope = inv_std * scale
+
     def activate(i, sums):
         at = pl.ds(pl.multiple_of(i * chunk, chunk), chunk)
-        normed = (zb[at] - group_mean) * inv_std
-        shifted = normed * scale + offset_
+        shifted = (zb[at] - group_mean) * slope + offset_
         gate = 1.0 / (1.0 + jnp.exp(-shifted))
         active = shifted * gate
-        pre = ab[at] * gate * (1.0 + shifted * (1.0 - gate))
-        zb[at] = normed
+        pre = ab[at] * (gate + active * (1.0 - gate))
+        zb[at] = shifted
         ab[at] = pre
         act[at] = active.astype(BF16)
         one = sums[0] + jnp.sum(pre, axis=0, keepdims=True)
-        two = sums[1] + jnp.sum(pre * normed, axis=0, keepdims=True)
+        two = sums[1] + jnp.sum(pre * shifted, axis=0, keepdims=True)
         return one, two
 
     zero = jnp.zeros((1, CMID), F32)
     sum_one, sum_two = lax.fori_loop(0, TH // rows, activate, (zero, zero))
+    rate = 1.0 / scale
+    sum_two = (sum_two - offset_ * sum_one) * rate
     ta[sp] = jnp.concatenate([sum_one, sum_two], axis=0)
     stage = share(ta, ta_send, ta_recv)
 
@@ -373,18 +376,20 @@
         def core_start(self, low, high):
             at = pl.ds(low, high - low)
             copy = send(self.p.at[1 - core, at], self.cc.at[at], *self.sems(), partner)
-            self.flight = self.flight + [copy]
+            self.flight = self.flight + [(copy, high // PIECE)]
 
         def core_finish(self):
-            arrive(self.flight)
-
             def body(j, carry):
                 value = self.p[core, self.span(j)] + self.cc[self.span(j)]
                 self.p[core, self.span(j)] = value
                 self.s[j] = value.astype(BF16)
                 return carry
 
-            lax.fori_loop(0, 16, body, 0)
+            done = 0
+            for copy, ready in self.flight:
+                arrive([copy])
+                lax.fori_loop(done, ready, body, 0)
+                done = ready
 
         def plane_start(self):
             self.flight = []
@@ -427,13 +432,14 @@
         def plane_back_start(self):
             at = self.ax.at[core, self.mine]
             self.flight = [(k, send(at, at, *self.sems(), at_plane(k))) for k in PLANE]
-            self.passed = [send(at, at, *self.sems(), partner)]
+            self.passed = []
 
         def plane_back_finish(self):
-            for k, copy in reversed(self.flight):
-                arrive([copy])
-                owner = lax.rem(y + 4 - k // 4, 4) * 4 + lax.rem(xx + 4 - k % 4, 4)
-                at = self.ax.at[core, owner]
+            flight = dict(self.flight)
+            for dy in (0, 1, 3, 2):
+                arrive([flight[k] for k in range(4 * dy, 4 * dy + 4) if k])
+                row = lax.rem(y + 4 - dy, 4)
+                at = self.ax.at[core, pl.ds(row * 4, 4)]
                 self.passed.append(send(at, at, *self.sems(), partner))
 
         def core_back_finish(self):
@@ -456,29 +462,30 @@
     one.plane_start()
     lax.fori_loop(7, 9, second_b, 0)
     two.core_start(640, 1152)
-    two.core_finish()
-    two.plane_start()
     arrive(stage)
     image_sums = jnp.sum(ta[...], axis=0)
     n = cells * GSIZE
     mean_shift = group_sum(scale * image_sums[0:1]) * (1.0 / n)
     mean_scale = group_sum(scale * image_sums[1:2]) * (1.0 / n)
 
+    by_shifted = inv_std * mean_scale * rate
+    by_one = inv_std * mean_shift - by_shifted * offset_
+
     def conv_grad(i, carry):
         at = pl.ds(pl.multiple_of(i * chunk, chunk), chunk)
-        value = (scale * ab[at] - mean_shift - zb[at] * mean_scale) * inv_std
-        value = value.astype(BF16)
-        c0[pl.ds(i * rows, rows)] = value.reshape(rows, TW, CMID)
-        cgf[pl.ds(i * rows, rows), 0:TW, :] = value.astype(F32).reshape(rows, TW, CMID)
+        value = ab[at] * slope - zb[at] * by_shifted - by_one
+        c0[pl.ds(i * rows, rows)] = value.astype(BF16).reshape(rows, TW, CMID)
         return carry
 
     lax.fori_loop(0, TH // rows, conv_grad, 0)
-    cs[...] = cgf[0:TH, 0:1, :]
+    cs[...] = c0[0:TH, 0:16, :].astype(F32)[:, 0:1, :]
     error = [
         send(cs, cr.at[pl.ds(0, TH)], c_send.at[0], c_recv.at[0], at_space(-1)),
         send(cs.at[0], cr.at[TH], c_send.at[1], c_recv.at[1], at_space(-5)),
         send(c0.at[0], c0.at[TH], c_send.at[2], c_recv.at[2], at_space(-4)),
     ]
+    two.core_finish()
+    two.plane_start()
     ux[xx] = image_sums
     share_x = [
         send(ux.at[xx], ux.at[xx], ux_send.at[k], ux_recv.at[k], at_plane(k)) for k in range(1, 4)
@@ -492,6 +499,14 @@
         first_wgrad(a)
         three.core_start(a * 384, a * 384 + 384)
 
+    def widen_c(i, carry):
+        at = pl.ds(4 * i, 4)
+        cgf[at, 0:TW, :] = c0[at].astype(F32)
+        return carry
+
+    lax.fori_loop(0, TH // 4, widen_c, 0)
+    three.core_finish()
+    three.plane_start()
     arrive(error)
     below = jnp.where(last_row, 0.0, c0[TH].astype(F32))
     c0[TH] = below.astype(BF16)
@@ -526,8 +541,6 @@
         ig[pl.ds(2 * p, 2 * rows)] = igf[...].astype(BF16)
         return carry
 
-    three.core_finish()
-    three.plane_start()
     one.plane_finish()
     one.z_start()
     arrive(share_x)
@@ -563,7 +576,7 @@
     one.plane_back_finish()
     three.z_back_finish()
     three.plane_back_start()
-    drained = len(pending) - 16
+    drained = len(pending) - 15
     two.plane_back_finish()
     one.core_back_finish()
     for copy in pending[:drained]:
@@ -669,7 +682,7 @@
             dma((6,)), dma((11,)), dma((11,)), dma((3,)), dma((3,)),
             dma((31,)), dma((31,)), dma((31,)), dma((31,)),
             dma((4,)), dma((4,)), dma((1,)), dma((1,)),
-            dma((63,)), dma((63,)), dma((63,)), dma((63,)), dma((63,)), dma((63,)),
+            dma((51,)), dma((51,)), dma((51,)), dma((51,)), dma((51,)), dma((51,)),
         ],
         compiler_params=pltpu.CompilerParams(
             collective_id=0, has_side_effects=True, vmem_limit_bytes=50 * 1024 * 1024

time: 71.4 us -> 69.4 us (0.972)
  Pallas kernels: 70.7 us -> 68.6 us
    pallas_call x1, Pallas kernels: 68.3 us -> 66.2 us  [on_device(): pl.pallas_call(kernel, out_shape=(vmem((2 * TH, 2 * TW, CIN), BF16), vmem...]
where the time goes in v3:
time: 69.4 us; the launch traced here: 69.3 us
  Pallas kernels  68.6 us (99%)
    pallas_call x1, Pallas kernels, on_device(): pl.pallas_call(kernel, out_shape=(vmem((2 * TH, 2 * TW, CIN), BF16), vmem...  66.2 us
    pallas_call x1, Pallas kernels, on_device(): pl.pallas_call(emit, out_shape=(jax.ShapeDtypeStruct((2 * TH, 2 * TW, CIN...  2.39 us

profile of v3, /device:TPU:1, one launch (start us, length us, event | category | flops | bytes accessed | tf_op | source)
XLA Modules:
  0.0 69.3 jit_solution(12828007627450150987)
XLA Ops:
  0.6 66.2 %shard_map.101 = (bf16[96,64,128]{2,1,0:T(8,128)(2,1)S(1)}, bf16[2,16,72,128]{3,2,1,0:T(8,128)(2,1)S(1)}, bf16[2,16,72,128]{3,2,1,0:T(8,128)(2,1)S(1)}, bf16[2,1...) custom-call(bf16[96,64,128]{2,1,0:T(8,128)(2,1)} %bitcast.11, bf16[3,384,256]{2,1,0:T(8,128)(2,1)} %bitcast.14, ...), custom_call_target="tpu_custom_call" | custom-call | tf_op jit(solution)/shard_map/pallas_call | solution.py:633
  66.9 2.4 %shard_map.102 = (bf16[96,64,128]{2,1,0:T(8,128)(2,1)}, f32[1152,256]{1,0:T(8,128)}, f32[2304,256]{1,0:T(8,128)}, f32[1,256]{1,0:T(1,128)}, f32[1,256]{1,0:T(1,128)}) custom-call(bf16[96,64,128]{2,1,0:T(8,128)(2,1)S(1)} %get-tuple-element.15.ig, bf16[2,16,72,128]{3,2,1,0:T(8,128)(2,1)S(1)} %get-tuple-element.16.axf, ...), custom_call_target="tpu_custom_call" | custom-call | tf_op jit(solution)/shard_map/pallas_call | solution.py:704

commit v4 on v3

--- a/solution.py
+++ b/solution.py
@@ -92,13 +92,17 @@
     partner = at_chip(xx, y, z, 1 - core)
 
     load_g = pltpu.make_async_copy(g_hbm, gs.at[1, pl.ds(1, TH)], in_sem.at[0])
-    load_x = pltpu.make_async_copy(x_hbm, x, in_sem.at[1])
+    load_x = [
+        pltpu.make_async_copy(x_hbm.at[at], x.at[at], in_sem.at[6 + i])
+        for i, at in enumerate(pl.ds(TH // 2 * i, TH // 2) for i in range(4))
+    ]
     load_w1 = pltpu.make_async_copy(w1_hbm, w1, in_sem.at[2])
     load_w2 = pltpu.make_async_copy(w2_hbm, w2, in_sem.at[3])
     load_gain = pltpu.make_async_copy(gain_hbm, gain, in_sem.at[4])
     load_bias = pltpu.make_async_copy(bias_hbm, bias, in_sem.at[5])
     load_g.start()
-    load_x.start()
+    for copy in load_x:
+        copy.start()
     load_w1.start()
     load_w2.start()
     load_gain.start()
@@ -140,7 +144,8 @@
     gfirst[...] = gf[1 : TH + 1, 8:9, :]
     glast[...] = gf[1 : TH + 1, 39:40, :]
 
-    load_x.wait()
+    for copy in load_x:
+        copy.wait()
     xe[...] = x[:, 56:64, :].astype(F32).reshape(16 * TH, CIN)
     xs[...] = xe[pl.ds(7, 2 * TH, stride=8), :]
     xsc[...] = xe[16 * TH - 1 : 16 * TH, :]
@@ -189,6 +194,10 @@
     load_w1.wait()
     rows = 8
     chunk = rows * TW
+    inner = slice(CIN, 3 * CIN)
+
+    def window(source, p, lanes):
+        return jnp.transpose(source[pl.ds(p, rows), :, lanes].reshape(chunk, -1))
 
     def first_conv(i, total):
         p = i * rows
@@ -201,6 +210,16 @@
         return total + jnp.sum(value, axis=0, keepdims=True)
 
     total = lax.fori_loop(0, TH // rows, first_conv, jnp.zeros((1, CMID), F32))
+
+    def turn_inner(i, carry):
+        at = pl.ds(pl.multiple_of(i * chunk, chunk), chunk)
+        p = i * rows
+        xt[0, inner, at] = window(ro, p, inner)
+        xt[1, inner, at] = window(re, p, inner)
+        xt[2, inner, at] = window(ro, p + 1, inner)
+        return carry
+
+    lax.fori_loop(0, TH // rows, turn_inner, 0)
 
     arrive(halo[0:3])
     xlf[0:1, :] = jnp.where(jnp.logical_or(first_col, first_row), 0.0, xlc[...])
@@ -283,14 +302,17 @@
     lax.fori_loop(0, TH // 4, left_x, 0)
     ro[TH, :, 0:CIN] = every_other(2 * TH, 7)
 
+    left = slice(0, CIN)
+
     def turn_x(i, carry):
         at = pl.ds(pl.multiple_of(i * chunk, chunk), chunk)
         p = i * rows
-        xt[0, :, at] = jnp.transpose(ro[pl.ds(p, rows)].reshape(chunk, 3 * CIN))
-        xt[1, :, at] = jnp.transpose(re[pl.ds(p, rows)].reshape(chunk, 3 * CIN))
-        xt[2, :, at] = jnp.transpose(ro[pl.ds(p + 1, rows)].reshape(chunk, 3 * CIN))
-        return carry
-
+        xt[0, left, at] = window(ro, p, left)
+        xt[1, left, at] = window(re, p, left)
+        xt[2, left, at] = window(ro, p + 1, left)
+        return carry
+
+    xt[0, inner, 0:chunk] = window(ro, 0, inner)
     lax.fori_loop(0, TH // rows, turn_x, 0)
 
     arrive(stage)
@@ -590,7 +612,9 @@
 
 def emit(ig, axf, axa, axb, one, out_ig, out1, out2, out_one, out_two, f1, f2, sem):
     copies = [
-        pltpu.make_async_copy(ig, out_ig, sem.at[0]),
+        pltpu.make_async_copy(ig.at[at], out_ig.at[at], sem.at[9 + i])
+        for i, at in enumerate(pl.ds(TH // 2 * i, TH // 2) for i in range(4))
+    ] + [
         pltpu.make_async_copy(one.at[0], out_one, sem.at[1]),
         pltpu.make_async_copy(one.at[1], out_two, sem.at[2]),
     ]
@@ -679,7 +703,7 @@
             vmem((4, 2, CMID), F32),
             vmem((2, 2, CMID), F32),
             *reduce_scratch,
-            dma((6,)), dma((11,)), dma((11,)), dma((3,)), dma((3,)),
+            dma((10,)), dma((11,)), dma((11,)), dma((3,)), dma((3,)),
             dma((31,)), dma((31,)), dma((31,)), dma((31,)),
             dma((4,)), dma((4,)), dma((1,)), dma((1,)),
             dma((51,)), dma((51,)), dma((51,)), dma((51,)), dma((51,)), dma((51,)),
@@ -715,7 +739,7 @@
         scratch_shapes=[
             vmem((9 * CIN, CMID), F32),
             vmem((9 * CMID, CMID), F32),
-            dma((9,)),
+            dma((13,)),
         ],
         compiler_params=pltpu.CompilerParams(vmem_limit_bytes=8 * 1024 * 1024),
     )(*inside)

time: 69.4 us -> 68.5 us (0.987)
  Pallas kernels: 68.6 us -> 67.7 us
    pallas_call x1, Pallas kernels: 66.2 us -> 65.3 us  [on_device(): pl.pallas_call(kernel, out_shape=(vmem((2 * TH, 2 * TW, CIN), BF16), vmem...]
where the time goes in v4:
time: 68.5 us; the launch traced here: 68.4 us
  Pallas kernels  67.7 us (99%)
    pallas_call x1, Pallas kernels, on_device(): pl.pallas_call(kernel, out_shape=(vmem((2 * TH, 2 * TW, CIN), BF16), vmem...  65.3 us
    pallas_call x1, Pallas kernels, on_device(): pl.pallas_call(emit, out_shape=(jax.ShapeDtypeStruct((2 * TH, 2 * TW, CIN...  2.43 us

profile of v4, /device:TPU:1, one launch (start us, length us, event | category | flops | bytes accessed | tf_op | source)
XLA Modules:
  0.0 68.4 jit_solution(10745843632735984630)
XLA Ops:
  0.6 65.3 %shard_map.101 = (bf16[96,64,128]{2,1,0:T(8,128)(2,1)S(1)}, bf16[2,16,72,128]{3,2,1,0:T(8,128)(2,1)S(1)}, bf16[2,16,72,128]{3,2,1,0:T(8,128)(2,1)S(1)}, bf16[2,1...) custom-call(bf16[96,64,128]{2,1,0:T(8,128)(2,1)} %bitcast.11, bf16[3,384,256]{2,1,0:T(8,128)(2,1)} %bitcast.14, ...), custom_call_target="tpu_custom_call" | custom-call | tf_op jit(solution)/shard_map/pallas_call | solution.py:657
  66.0 2.4 %shard_map.102 = (bf16[96,64,128]{2,1,0:T(8,128)(2,1)}, f32[1152,256]{1,0:T(8,128)}, f32[2304,256]{1,0:T(8,128)}, f32[1,256]{1,0:T(1,128)}, f32[1,256]{1,0:T(1,128)}) custom-call(bf16[96,64,128]{2,1,0:T(8,128)(2,1)S(1)} %get-tuple-element.15.ig, bf16[2,16,72,128]{3,2,1,0:T(8,128)(2,1)S(1)} %get-tuple-element.16.axf, ...), custom_call_target="tpu_custom_call" | custom-call | tf_op jit(solution)/shard_map/pallas_call | solution.py:728

commit v5 on v4

--- a/solution.py
+++ b/solution.py
@@ -40,13 +40,14 @@
 
 def kernel(
     x_hbm, w1_hbm, gain_hbm, bias_hbm, w2_hbm, g_hbm,
-    ig, axf, axa, axb, ogb,
+    ig, axf, og2, ogb,
     x, w1, w2, gain, bias,
     xe, xf, re, ro, xs, xsc, xl, xlc, xlf, xtop,
     gs, gf, gfirst, glast, rl, rr,
     zb, ab, act, act_t, xt,
     cgf, c0, c1, cs, cr, igf,
     sa, ta, ux, uz,
+    axa, axb,
     pa, ca, sta, rxa, qa, rza, aza,
     pb, cb, stb, rxb, qb, rzb, azb,
     pf, cf, stf, rxf, qf, rzf, azf,
@@ -529,6 +530,8 @@
     lax.fori_loop(0, TH // 4, widen_c, 0)
     three.core_finish()
     three.plane_start()
+    one.plane_finish()
+    one.z_start()
     arrive(error)
     below = jnp.where(last_row, 0.0, c0[TH].astype(F32))
     c0[TH] = below.astype(BF16)
@@ -563,8 +566,6 @@
         ig[pl.ds(2 * p, 2 * rows)] = igf[...].astype(BF16)
         return carry
 
-    one.plane_finish()
-    one.z_start()
     arrive(share_x)
     uz[z_lo] = slot_sum(ux, 4)
     share_z = [
@@ -599,43 +600,53 @@
     three.z_back_finish()
     three.plane_back_start()
     drained = len(pending) - 15
+
+    def widen_second(ax, base, j):
+        at = pl.ds(pl.multiple_of((base + j) * PIECE, 8), PIECE)
+        og2[at, 0:128] = ax[0, j].astype(F32)
+        og2[at, 128:256] = ax[1, j].astype(F32)
+        return 0
+
     two.plane_back_finish()
     one.core_back_finish()
+    lax.fori_loop(0, 16, lambda j, carry: widen_second(axa, 0, j), 0)
     for copy in pending[:drained]:
         copy.wait_send()
+    two.core_back_finish()
+    lax.fori_loop(0, 16, lambda j, carry: widen_second(axb, 16, j), 0)
     three.plane_back_finish()
-    two.core_back_finish()
     three.core_back_finish()
     for copy in pending[drained:]:
         copy.wait_send()
 
 
-def emit(ig, axf, axa, axb, one, out_ig, out1, out2, out_one, out_two, f1, f2, sem):
-    copies = [
-        pltpu.make_async_copy(ig.at[at], out_ig.at[at], sem.at[9 + i])
-        for i, at in enumerate(pl.ds(TH // 2 * i, TH // 2) for i in range(4))
-    ] + [
-        pltpu.make_async_copy(one.at[0], out_one, sem.at[1]),
-        pltpu.make_async_copy(one.at[1], out_two, sem.at[2]),
-    ]
-    for copy in copies:
+def emit(ig, axf, og2, one, out_ig, out1, out2, out_one, out_two, f1, sem):
+    copies = []
+
+    def start(source, target):
+        copy = pltpu.make_async_copy(source, target, sem.at[len(copies)])
         copy.start()
-    at = 3
-    for ax, full, out, base in ((axa, f2, out2, 0), (axb, f2, out2, 16), (axf, f1, out1, 0)):
-
-        def widen(j, carry):
-            rows = pl.ds(pl.multiple_of((base + j) * PIECE, 8), PIECE)
-            full[rows, 0:128] = ax[0, j].astype(F32)
-            full[rows, 128:256] = ax[1, j].astype(F32)
-            return carry
-
-        for half in range(2):
-            lax.fori_loop(8 * half, 8 * half + 8, widen, 0)
-            rows = pl.ds((base + 8 * half) * PIECE, 8 * PIECE)
-            copy = pltpu.make_async_copy(full.at[rows], out.at[rows], sem.at[at])
-            copy.start()
-            copies.append(copy)
-            at += 1
+        copies.append(copy)
+
+    start(one.at[0], out_one)
+    start(one.at[1], out_two)
+    for i in range(4):
+        at = pl.ds(9 * CMID // 4 * i, 9 * CMID // 4)
+        start(og2.at[at], out2.at[at])
+    for i in range(4):
+        at = pl.ds(TH // 2 * i, TH // 2)
+        start(ig.at[at], out_ig.at[at])
+
+    def widen(j, carry):
+        rows = pl.ds(pl.multiple_of(j * PIECE, 8), PIECE)
+        f1[rows, 0:128] = axf[0, j].astype(F32)
+        f1[rows, 128:256] = axf[1, j].astype(F32)
+        return carry
+
+    for half in range(2):
+        lax.fori_loop(8 * half, 8 * half + 8, widen, 0)
+        rows = pl.ds(8 * half * PIECE, 8 * PIECE)
+        start(f1.at[rows], out1.at[rows])
     for copy in copies:
         copy.wait()
 
@@ -659,12 +670,11 @@
         out_shape=(
             vmem((2 * TH, 2 * TW, CIN), BF16),
             vmem((2, 16, PIECE, 128), BF16),
-            vmem((2, 16, PIECE, 128), BF16),
-            vmem((2, 16, PIECE, 128), BF16),
+            vmem((9 * CMID, CMID), F32),
             vmem((2, 1, CMID), F32),
         ),
         in_specs=[outside] * 6,
-        out_specs=(whole,) * 5,
+        out_specs=(whole,) * 4,
         scratch_shapes=[
             vmem((2 * TH, 2 * TW, CIN), BF16),
             vmem((3, 3 * CIN, CMID), BF16),
@@ -702,6 +712,8 @@
             vmem((TILES, 2, CMID), F32),
             vmem((4, 2, CMID), F32),
             vmem((2, 2, CMID), F32),
+            vmem((2, 16, PIECE, 128), BF16),
+            vmem((2, 16, PIECE, 128), BF16),
             *reduce_scratch,
             dma((10,)), dma((11,)), dma((11,)), dma((3,)), dma((3,)),
             dma((31,)), dma((31,)), dma((31,)), dma((31,)),
@@ -734,12 +746,11 @@
             jax.ShapeDtypeStruct((1, CMID), F32),
             jax.ShapeDtypeStruct((1, CMID), F32),
         ),
-        in_specs=[whole] * 5,
+        in_specs=[whole] * 4,
         out_specs=(outside,) * 5,
         scratch_shapes=[
             vmem((9 * CIN, CMID), F32),
-            vmem((9 * CMID, CMID), F32),
-            dma((13,)),
+            dma((12,)),
         ],
         compiler_params=pltpu.CompilerParams(vmem_limit_bytes=8 * 1024 * 1024),
     )(*inside)

time: 68.5 us -> 68.1 us (level)
  no operation moved by 1% of the time
where the time goes in v5:
time: 68.1 us; the launch traced here: 68 us
  Pallas kernels  67.3 us (99%)
    pallas_call x1, Pallas kernels, on_device(): pl.pallas_call(kernel, out_shape=(vmem((2 * TH, 2 * TW, CIN), BF16), vmem...  64.9 us
    pallas_call x1, Pallas kernels, on_device(): pl.pallas_call(emit, out_shape=(jax.ShapeDtypeStruct((2 * TH, 2 * TW, CIN...  2.42 us

profile of v5, /device:TPU:1, one launch (start us, length us, event | category | flops | bytes accessed | tf_op | source)
XLA Modules:
  0.0 68.0 jit_solution(1330198966091297368)
XLA Ops:
  0.6 64.9 %shard_map.101 = (bf16[96,64,128]{2,1,0:T(8,128)(2,1)S(1)}, bf16[2,16,72,128]{3,2,1,0:T(8,128)(2,1)S(1)}, f32[2304,256]{1,0:T(8,128)S(1)}, f32[2,1,256]{2,1,0:T(1,128)S(1)}) custom-call(bf16[96,64,128]{2,1,0:T(8,128)(2,1)} %bitcast.11, bf16[3,384,256]{2,1,0:T(8,128)(2,1)} %bitcast.14, f32[1,256]{1,0:T(1,128)} %bitcast.15, f32[1,256]{1,0:T(1,128)} %bitcast.16, ...), custom_call_target="tpu_custom_call" | custom-call | tf_op jit(solution)/shard_map/pallas_call | solution.py:668
  65.5 2.4 %shard_map.102 = (bf16[96,64,128]{2,1,0:T(8,128)(2,1)}, f32[1152,256]{1,0:T(8,128)}, f32[2304,256]{1,0:T(8,128)}, f32[1,256]{1,0:T(1,128)}, f32[1,256]{1,0:T(1,128)}) custom-call(bf16[96,64,128]{2,1,0:T(8,128)(2,1)S(1)} %get-tuple-element.14.ig, bf16[2,16,72,128]{3,2,1,0:T(8,128)(2,1)S(1)} %get-tuple-element.15.axf, f32[2304,256]{1,0:T(8,128)S(1)} %get-tuple-element.16.og2, ...), custom_call_target="tpu_custom_call" | custom-call | tf_op jit(solution)/shard_map/pallas_call | solution.py:740

commit v6 on v4

--- a/solution.py
+++ b/solution.py
@@ -529,6 +529,8 @@
     lax.fori_loop(0, TH // 4, widen_c, 0)
     three.core_finish()
     three.plane_start()
+    one.plane_finish()
+    one.z_start()
     arrive(error)
     below = jnp.where(last_row, 0.0, c0[TH].astype(F32))
     c0[TH] = below.astype(BF16)
@@ -563,8 +565,6 @@
         ig[pl.ds(2 * p, 2 * rows)] = igf[...].astype(BF16)
         return carry
 
-    one.plane_finish()
-    one.z_start()
     arrive(share_x)
     uz[z_lo] = slot_sum(ux, 4)
     share_z = [
@@ -595,10 +595,10 @@
     sums = slot_sum(uz, 2)
     ogb[0] = sums[0:1]
     ogb[1] = sums[1:2]
-    one.plane_back_finish()
     three.z_back_finish()
     three.plane_back_start()
     drained = len(pending) - 15
+    one.plane_back_finish()
     two.plane_back_finish()
     one.core_back_finish()
     for copy in pending[:drained]:

time: 68.5 us -> 68.2 us (level)
  no operation moved by 1% of the time
where the time goes in v6:
time: 68.2 us
  Pallas kernels  67.5 us (99%)
    pallas_call x1, Pallas kernels, on_device(): pl.pallas_call(kernel, out_shape=(vmem((2 * TH, 2 * TW, CIN), BF16), vmem...  65.1 us
    pallas_call x1, Pallas kernels, on_device(): pl.pallas_call(emit, out_shape=(jax.ShapeDtypeStruct((2 * TH, 2 * TW, CIN...  2.43 us

profile of v6, /device:TPU:1, one launch (start us, length us, event | category | flops | bytes accessed | tf_op | source)
XLA Modules:
  0.0 68.2 jit_solution(15899901318925379800)
XLA Ops:
  0.6 65.1 %shard_map.101 = (bf16[96,64,128]{2,1,0:T(8,128)(2,1)S(1)}, bf16[2,16,72,128]{3,2,1,0:T(8,128)(2,1)S(1)}, bf16[2,16,72,128]{3,2,1,0:T(8,128)(2,1)S(1)}, bf16[2,1...) custom-call(bf16[96,64,128]{2,1,0:T(8,128)(2,1)} %bitcast.11, bf16[3,384,256]{2,1,0:T(8,128)(2,1)} %bitcast.14, ...), custom_call_target="tpu_custom_call" | custom-call | tf_op jit(solution)/shard_map/pallas_call | solution.py:657
  65.7 2.4 %shard_map.102 = (bf16[96,64,128]{2,1,0:T(8,128)(2,1)}, f32[1152,256]{1,0:T(8,128)}, f32[2304,256]{1,0:T(8,128)}, f32[1,256]{1,0:T(1,128)}, f32[1,256]{1,0:T(1,128)}) custom-call(bf16[96,64,128]{2,1,0:T(8,128)(2,1)S(1)} %get-tuple-element.15.ig, bf16[2,16,72,128]{3,2,1,0:T(8,128)(2,1)S(1)} %get-tuple-element.16.axf, ...), custom_call_target="tpu_custom_call" | custom-call | tf_op jit(solution)/shard_map/pallas_call | solution.py:728

commit v7 on v6

--- a/solution.py
+++ b/solution.py
@@ -581,7 +581,7 @@
     one.z_back_start()
     three.plane_finish()
     three.z_start()
-    lax.fori_loop(3, 5, up_conv, 0)
+    lax.fori_loop(3, 6, up_conv, 0)
     two.z_finish()
     two.z_back_start()
     one.z_back_finish()
@@ -590,7 +590,6 @@
     three.z_back_start()
     two.z_back_finish()
     two.plane_back_start()
-    lax.fori_loop(5, 6, up_conv, 0)
     arrive(share_z)
     sums = slot_sum(uz, 2)
     ogb[0] = sums[0:1]

time: 68.2 us -> 68.2 us (level)
  no operation moved by 1% of the time
where the time goes in v7:
time: 68.2 us
  Pallas kernels  67.5 us (99%)
    pallas_call x1, Pallas kernels, on_device(): pl.pallas_call(kernel, out_shape=(vmem((2 * TH, 2 * TW, CIN), BF16), vmem...  65.1 us
    pallas_call x1, Pallas kernels, on_device(): pl.pallas_call(emit, out_shape=(jax.ShapeDtypeStruct((2 * TH, 2 * TW, CIN...  2.43 us

profile of v7, /device:TPU:1, one launch (start us, length us, event | category | flops | bytes accessed | tf_op | source)
XLA Modules:
  0.0 68.2 jit_solution(8011339347361253257)
XLA Ops:
  0.6 65.1 %shard_map.101 = (bf16[96,64,128]{2,1,0:T(8,128)(2,1)S(1)}, bf16[2,16,72,128]{3,2,1,0:T(8,128)(2,1)S(1)}, bf16[2,16,72,128]{3,2,1,0:T(8,128)(2,1)S(1)}, bf16[2,1...) custom-call(bf16[96,64,128]{2,1,0:T(8,128)(2,1)} %bitcast.11, bf16[3,384,256]{2,1,0:T(8,128)(2,1)} %bitcast.14, ...), custom_call_target="tpu_custom_call" | custom-call | tf_op jit(solution)/shard_map/pallas_call | solution.py:656
  65.7 2.4 %shard_map.102 = (bf16[96,64,128]{2,1,0:T(8,128)(2,1)}, f32[1152,256]{1,0:T(8,128)}, f32[2304,256]{1,0:T(8,128)}, f32[1,256]{1,0:T(1,128)}, f32[1,256]{1,0:T(1,128)}) custom-call(bf16[96,64,128]{2,1,0:T(8,128)(2,1)S(1)} %get-tuple-element.15.ig, bf16[2,16,72,128]{3,2,1,0:T(8,128)(2,1)S(1)} %get-tuple-element.16.axf, ...), custom_call_target="tpu_custom_call" | custom-call | tf_op jit(solution)/shard_map/pallas_call | solution.py:727
